TPU v7x, 256 devices: a whole 4x4x8 slice. The times are simulated.
256 devices in a mesh: gy: 32 (over x_hi, z, core), gz: 8 (over x_lo, y).
Axes of the slice: x: 4 (x_hi: 2, x_lo: 2; x = x_hi * 2 + x_lo), y: 4, z: 8, core: 2. Of those that a mesh axis runs over, the one named last changes fastest.
Arguments:
- populations: float32 [19, 4, 256, 8192], P(None, None, 'gy', 'gz'), may hold values from 0 to 1, as said below
- solid_mask: int32 [4, 256, 8192], P(None, 'gy', 'gz'), may hold values 0 or 1
- body_force: float32 [3], replicated, may hold values from 0.002 to 0.008
Outputs:
- density: float32 [4, 256, 8192], P(None, 'gy', 'gz')
- velocity: float32 [3, 4, 256, 8192], P(None, None, 'gy', 'gz')
Inputs may be any that keep to these rules, and one draw needn't show every extreme that they name: `populations`: every population is positive, near its lattice weight times one.
All inputs are finite; a program needn't handle non-finite values. No bound on the sum of `solid_mask` on one device may be relied on, other than what follows from the above.
Results may differ from a plain program's by a relative error of at most 0.0003.
Values sent between devices are 32-bit elements; how exact they have to be, the bound alone decides.
No kernel may reach another device: no remote copies, remote signals or barrier semaphores. Data moves between devices by JAX's collectives and lax.ppermute only.
A program may use at most 64 MiB of HBM per device.

v0:
```python
import jax
import jax.numpy as jnp
from jax import lax
from jax.experimental import pallas as pl
from jax.experimental.pallas import tpu as pltpu
from jax.sharding import PartitionSpec as P

VEL = [
    (0, 0, 0),
    (1, 0, 0),
    (-1, 0, 0),
    (0, 1, 0),
    (0, -1, 0),
    (0, 0, 1),
    (0, 0, -1),
    (1, 1, 0),
    (-1, -1, 0),
    (1, -1, 0),
    (-1, 1, 0),
    (1, 0, 1),
    (-1, 0, -1),
    (1, 0, -1),
    (-1, 0, 1),
    (0, 1, 1),
    (0, -1, -1),
    (0, 1, -1),
    (0, -1, 1),
]
OPP = [VEL.index((-x, -y, -z)) for x, y, z in VEL]
FLIP = [VEL.index((x, -y, z)) for x, y, z in VEL]
IN = [k for k in range(19) if VEL[k][1] == 1]
OUT = [FLIP[k] for k in IN]
FLAT = [k for k in range(19) if VEL[k][1] == 0]
LOCAL = FLAT + OUT
NMSG = 24
MACH = 0.05
BIG = 1e30
NAN = float("nan")
F32 = jnp.float32


def lanes():
    return lax.broadcasted_iota(jnp.int32, (8, 128), 1)


def rows():
    return lax.broadcasted_iota(jnp.int32, (8, 128), 0)


def collide(f, force):
    fx, fy, fz = force
    sx, dx = f[1] + f[2], f[1] - f[2]
    sy, dy = f[3] + f[4], f[3] - f[4]
    sz, dz = f[5] + f[6], f[5] - f[6]

    def plane(a):
        big, small = f[a] + f[a + 1], f[a] - f[a + 1]
        big2, small2 = f[a + 2] + f[a + 3], f[a + 2] - f[a + 3]
        return big + big2, big - big2, small + small2, small - small2

    nxy, mxy, tyyx, txxy = plane(7)
    nxz, mxz, tzzx, txxz = plane(11)
    nyz, myz, tzzy, tyyz = plane(15)
    jx = dx + (tyyx + tzzx)
    jy = dy + (txxy + tzzy)
    jz = dz + (txxz + tyyz)
    mxx = sx + (nxy + nxz)
    myy = sy + (nxy + nyz)
    mzz = sz + (nxz + nyz)
    rho = ((f[0] + mxx) + (sy + sz)) + nyz
    inv = 0.3125 / rho
    vx, vy, vz = jx * inv, jy * inv, jz * inv
    gx, gy, gz = jx * vx, jy * vy, jz * vz
    third = rho * (1.25 / 6.0)
    hx = (third + (gx + gx)) - 0.125 * mxx
    hy = (third + (gy + gy)) - 0.125 * myy
    hz = (third + (gz + gz)) - 0.125 * mzz
    mxy = jx * vy - 0.0625 * mxy
    mxz = jx * vz - 0.0625 * mxz
    myz = jy * vz - 0.0625 * myz
    base = rho * (1.3 / 36.0) + (gx + gy + gz) * (1.3 / 12.0 / 0.3125)
    nxy = (base - 0.52 * gz) - 0.075 * nxy
    nxz = (base - 0.52 * gy) - 0.075 * nxz
    nyz = (base - 0.52 * gx) - 0.075 * nyz
    bx = jx * (0.4 / 3.0) + fx * (1.0 / 12.0)
    by = jy * (0.4 / 3.0) + fy * (1.0 / 12.0)
    bz = jz * (0.4 / 3.0) + fz * (1.0 / 12.0)
    tyyx, tzzx = bx - 0.15 * tyyx, bx - 0.15 * tzzx
    txxy, tzzy = by - 0.15 * txxy, by - 0.15 * tzzy
    txxz, tyyz = bz - 0.15 * txxz, bz - 0.15 * tyyz
    out = [None] * 19

    def axis(a, half, j, force_a, n1, n2, t1, t2):
        even = half - 2.0 * (n1 + n2)
        odd = 0.5 * (j + force_a) - 2.0 * (t1 + t2)
        out[a], out[a + 1] = even + odd, even - odd

    def edge(a, n, m, t1, t2):
        big, big2 = n + m, n - m
        small, small2 = t1 + t2, t1 - t2
        out[a], out[a + 1] = big + small, big - small
        out[a + 2], out[a + 3] = big2 + small2, big2 - small2

    axis(1, hx, jx, fx, nxy, nxz, tyyx, tzzx)
    axis(3, hy, jy, fy, nxy, nyz, txxy, tzzy)
    axis(5, hz, jz, fz, nxz, nyz, txxz, tyyz)
    edge(7, nxy, mxy, tyyx, txxy)
    edge(11, nxz, mxz, tzzx, txxz)
    edge(15, nyz, myz, tzzy, tyyz)
    out[0] = rho - 2.0 * (hx + hy + hz) + 4.0 * (nxy + nxz + nyz)
    return out


def along_z(get, t, cz, lane):
    cur = get(t)
    if cz == 0:
        return cur
    if cz == 1:
        before = get(jnp.where(t == 0, 8, t - 1))
        return pltpu.roll(jnp.where(lane == 127, before, cur), 1, axis=1)
    after = get(jnp.where(t == 8, 0, t + 1))
    return pltpu.roll(jnp.where(lane == 0, after, cur), 127, axis=1)


def stream_own(ref, halo, p, t, lane, row):
    f = []
    for k in range(19):
        cx, cy, cz = VEL[k]
        own = ref[OPP[k], t, 8 * p : 8 * p + 8, :]
        q = p - cx
        if k == 0 or q < 0 or q > 3:
            f.append(own)
            continue

        def get(s, k=k, q=q, cy=cy):
            v = ref[k, s, 8 * q : 8 * q + 8, :]
            if cy == 0 or halo is None:
                return v
            if cy == 1:
                at, i, sub = 7, IN.index(k), q
            else:
                at, i, sub = 0, IN.index(FLIP[k]), 4 + q
            rim = jnp.broadcast_to(halo[i, s, sub : sub + 1, :], (8, 128))
            return jnp.where(row == at, rim, v)

        v = along_z(get, t, cz, lane)
        if cy == 1:
            v = pltpu.roll(v, 1, axis=0)
        elif cy == -1:
            v = pltpu.roll(v, 7, axis=0)
        f.append(jnp.where(v < BIG, v, own))
    return f


def stream_rim(get, own, k, t, lane, row):
    cx, _, cz = VEL[k]
    v = along_z(get, t, cz, lane)
    if cx:
        v = pltpu.roll(v, cx % 8, axis=0)
        wall = (row & 3) == (0 if cx == 1 else 3)
        v = jnp.where(wall, NAN, v)
    return jnp.where(v < BIG, v, own)


def edges(ref, k, t, lower, upper):
    a = ref[k, t, pl.ds(lower, 4, stride=8), :]
    b = ref[FLIP[k], t, pl.ds(upper, 4, stride=8), :]
    return jnp.concatenate([a, b], axis=0)


def force_of(force_ref):
    return force_ref[0], force_ref[1], force_ref[2]


def rim_force(force, row):
    fx, fy, fz = force
    return fx, jnp.where(row < 4, fy, -fy), fz


def pack_kernel(first, last, mask_first, mask_last, out0, out1):
    lane = lanes()
    even = lax.rem(lax.axis_index("gz"), 2) == 0
    group = lane // 4
    for tile in range(3):
        left = jnp.zeros((8, 128), F32)
        right = jnp.zeros((8, 128), F32)
        for s in range(32):
            i = tile * 32 + s
            if i >= 76:
                break
            k, p = i // 4, i % 4
            a, b = first[k, p], last[k, p]
            if k == 0:
                a = jnp.where(mask_first[p] > 0, NAN, a)
                b = jnp.where(mask_last[p] > 0, NAN, b)
            if s:
                a = pltpu.roll(a, 4 * s, axis=1)
            if s != 31:
                b = pltpu.roll(b, 4 * s + 4, axis=1)
            left = jnp.where(group == s, a, left)
            right = jnp.where(group == s, b, right)
        out0[tile] = jnp.where(even, right, left)
        out1[tile] = jnp.where(even, left, right)


def first_kernel(force_ref, pop, mask, got0, got1, r2, edge, near, far, r1, f1, rim):
    lane, row = lanes(), rows()
    force = force_of(force_ref)
    even_z = lax.rem(lax.axis_index("gz"), 2) == 0
    even_y = lax.rem(lax.axis_index("gy"), 2) == 0
    for tile in range(3):
        a, b = got0[tile], got1[tile]
        from_right = jnp.where(even_z, a, b)
        from_left = jnp.where(even_z, b, a)
        for s in range(32):
            i = tile * 32 + s
            if i >= 76:
                break
            k, p = i // 4, i % 4
            x = pltpu.roll(from_right, 128 - 4 * s, axis=1) if s else from_right
            y = pltpu.roll(from_left, 124 - 4 * s, axis=1) if s != 31 else from_left
            rim[k, p] = jnp.where(lane < 64, x, y)

    def put(t, p, f):
        g = collide(f, force)
        for k in range(19):
            r1[k, t, 8 * p : 8 * p + 8, :] = g[k]

    @pl.loop(0, 8)
    def _(t):
        at = pl.ds(pl.multiple_of(t * 128, 128), 128)
        for p in range(4):
            f = [pop[k, p, :, at] for k in range(19)]
            f[0] = jnp.where(mask[p, :, at] > 0, NAN, f[0])
            put(t, p, f)

    for p in range(4):
        put(8, p, [rim[k, p] for k in range(19)])

    @pl.loop(0, 9)
    def _(t):
        for p in range(4):
            f = stream_own(r1, None, p, t, lane, row)
            for k in range(19):
                f1[k, t, 8 * p : 8 * p + 8, :] = f[k]
            g = collide(f, force)
            for k in range(19):
                r2[k, t, 8 * p : 8 * p + 8, :] = g[k]

    @pl.loop(0, 9)
    def _(t):
        values = [edges(r1, k, t, 0, 7) for k in OUT]
        values += [edges(f1, k, t, 0, 7) for k in LOCAL]
        values += [edges(r2, k, t, 1, 6) for k in OUT]
        for i, v in enumerate(values):
            edge[i, t] = v
            w = jnp.where(even_y, pltpu.roll(v, 4, axis=0), v)
            near[i, t] = w[0:4]
            far[i, t] = w[4:8]


def last_kernel(
    force_ref, r2_hbm, edge, near, far, mask, density, velocity, r2, r3, got, r2h, r2e, r3h, sem
):
    copy = pltpu.make_async_copy(r2_hbm, r2, sem)
    copy.start()
    lane, row = lanes(), rows()
    force = force_of(force_ref)
    force_rim = rim_force(force, row)
    even_y = lax.rem(lax.axis_index("gy"), 2) == 0

    @pl.loop(0, 9)
    def _(t):
        for i in range(NMSG):
            v = jnp.concatenate([near[i, t], far[i, t]], axis=0)
            got[i, t] = jnp.where(even_y, pltpu.roll(v, 4, axis=0), v)

    copy.wait()

    @pl.loop(0, 9)
    def _(t):
        f = [None] * 19
        for i, k in enumerate(LOCAL):
            f[k] = edge[5 + i, t]
        for i, k in enumerate(IN):
            own = edge[OUT.index(OPP[k]), t]
            f[k] = stream_rim(lambda s, i=i: got[i, s], own, k, t, lane, row)
        g = collide(f, force_rim)
        for k in range(19):
            r2[k, t, pl.ds(0, 4, stride=8), :] = g[k][0:4]
            r2[FLIP[k], t, pl.ds(7, 4, stride=8), :] = g[k][4:8]
        for i, k in enumerate(OUT):
            r2e[i, t] = g[k]
        f = [None] * 19
        for i, k in enumerate(LOCAL):
            f[FLIP[k]] = got[5 + i, t]
        for i, k in enumerate(OUT):
            own = got[IN.index(OPP[k]), t]
            f[k] = stream_rim(lambda s, i=i: edge[i, s], own, k, t, lane, row)
        g = collide(f, force_rim)
        for i, k in enumerate(IN + FLAT + OUT):
            r2h[i, t] = g[k]

    place = {k: i for i, k in enumerate(IN + FLAT + OUT)}

    @pl.loop(0, 9)
    def _(t):
        f = [None] * 19
        for k in range(19):
            own = r2h[place[OPP[k]], t]
            if k == 0:
                f[k] = own
            elif k in FLAT:
                f[k] = stream_rim(lambda s, k=k: r2h[place[k], s], own, k, t, lane, row)
            elif k in IN:
                f[k] = stream_rim(lambda s, k=k: got[19 + IN.index(k), s], own, k, t, lane, row)
            else:
                f[k] = stream_rim(lambda s, k=k: r2e[OUT.index(k), s], own, k, t, lane, row)
        g = collide(f, force_rim)
        for i, k in enumerate(IN):
            r3h[i, t] = g[k]
        for p in range(4):
            g = collide(stream_own(r2, r2h, p, t, lane, row), force)
            for k in range(19):
                r3[k, t, 8 * p : 8 * p + 8, :] = g[k]

    @pl.loop(0, 8)
    def _(t):
        at = pl.ds(pl.multiple_of(t * 128, 128), 128)
        for p in range(4):
            f = stream_own(r3, r3h, p, t, lane, row)
            rho = f[0]
            for k in range(1, 19):
                rho = rho + f[k]
            solid = mask[p, :, at] > 0
            density[p, :, at] = jnp.where(solid, 0.0, rho)
            inv = (1.0 / MACH) / rho
            for a in range(3):
                plus = [f[k] for k in range(19) if VEL[k][a] == 1]
                minus = [f[k] for k in range(19) if VEL[k][a] == -1]
                j = plus[0] - minus[0]
                for x, y in zip(plus[1:], minus[1:]):
                    j = j + (x - y)
                velocity[a, p, :, at] = jnp.where(solid, 0.0, j * inv)


VMEM = pl.BlockSpec(memory_space=pltpu.VMEM)
SMEM = pl.BlockSpec(memory_space=pltpu.SMEM)
ANY = pl.BlockSpec(memory_space=pl.ANY)


def params():
    return pltpu.CompilerParams(vmem_limit_bytes=48 * 1024 * 1024)


def sds(*shape):
    return jax.ShapeDtypeStruct(shape, F32)


def swap(x, axis, parity):
    count = lax.axis_size(axis)
    pairs = [(i, (i + 1) % count if i % 2 == parity else (i - 1) % count) for i in range(count)]
    return lax.ppermute(x, axis, pairs)


def local(pop, mask, force):
    z0, z1 = pl.pallas_call(
        pack_kernel,
        out_shape=(sds(3, 8, 128), sds(3, 8, 128)),
        grid=(1,),
        in_specs=[
            pl.BlockSpec((19, 4, 8, 128), lambda i: (0, 0, 0, 0)),
            pl.BlockSpec((19, 4, 8, 128), lambda i: (0, 0, 0, 7)),
            pl.BlockSpec((4, 8, 128), lambda i: (0, 0, 0)),
            pl.BlockSpec((4, 8, 128), lambda i: (0, 0, 7)),
        ],
        out_specs=(
            pl.BlockSpec((3, 8, 128), lambda i: (0, 0, 0)),
            pl.BlockSpec((3, 8, 128), lambda i: (0, 0, 0)),
        ),
        compiler_params=params(),
        name="pack",
    )(pop, pop, mask, mask)
    got0 = swap(z0, "gz", 0)
    got1 = swap(z1, "gz", 1)
    r2, edge, near, far = pl.pallas_call(
        first_kernel,
        out_shape=(sds(19, 9, 32, 128), sds(NMSG, 9, 8, 128), sds(NMSG, 9, 4, 128), sds(NMSG, 9, 4, 128)),
        in_specs=[SMEM, VMEM, VMEM, VMEM, VMEM],
        out_specs=(VMEM, VMEM, VMEM, VMEM),
        scratch_shapes=[
            pltpu.VMEM((19, 9, 32, 128), F32),
            pltpu.VMEM((19, 9, 32, 128), F32),
            pltpu.VMEM((19, 4, 8, 128), F32),
        ],
        compiler_params=params(),
        name="first",
    )(force, pop, mask, got0, got1)
    far = swap(far, "gy", 1)
    near = swap(near, "gy", 0)
    return pl.pallas_call(
        last_kernel,
        out_shape=(sds(4, 8, 1024), sds(3, 4, 8, 1024)),
        in_specs=[SMEM, ANY, VMEM, VMEM, VMEM, VMEM],
        out_specs=(VMEM, VMEM),
        scratch_shapes=[
            pltpu.VMEM((19, 9, 32, 128), F32),
            pltpu.VMEM((19, 9, 32, 128), F32),
            pltpu.VMEM((NMSG, 9, 8, 128), F32),
            pltpu.VMEM((19, 9, 8, 128), F32),
            pltpu.VMEM((5, 9, 8, 128), F32),
            pltpu.VMEM((5, 9, 8, 128), F32),
            pltpu.SemaphoreType.DMA,
        ],
        compiler_params=params(),
        name="last",
    )(force, r2, edge, near, far, mask)


def solution(mesh):
    return jax.shard_map(
        local,
        mesh=mesh,
        in_specs=(P(None, None, "gy", "gz"), P(None, "gy", "gz"), P()),
        out_specs=(P(None, "gy", "gz"), P(None, None, "gy", "gz")),
        check_vma=False,
    )
```

profile of v0, /device:TPU:24, one launch (start us, length us, event | category | flops | bytes accessed | tf_op | source)
XLA Modules:
  0.0 37.9 jit_solution(7149836643850954503)
XLA Ops:
  0.6 0.0 copy-start
  0.6 1.7 %copy-done = f32[19,4,8,1024]{3,2,1,0:T(8,128)S(1)} copy-done((f32[19,4,8,1024]{3,2,1,0:T(8,128)S(1)}, f32[19,4,8,1024]{3,2,1,0:T(8,128)}, u32[]{:S(2)}) %copy-start) | copy-done | bytes 2490392
  2.3 0.0 copy-start.2
  2.3 0.9 %copy-done.2 = s32[4,8,1024]{2,1,0:T(8,128)S(1)} copy-done((s32[4,8,1024]{2,1,0:T(8,128)S(1)}, s32[4,8,1024]{2,1,0:T(8,128)}, u32[]{:S(2)}) %copy-start.2) | copy-done | bytes 131096
  3.2 0.0 copy-start.4
  3.2 0.0 copy-start.3
  3.2 0.2 pack.1
  3.5 0.8 %collective-permute-start = (f32[3,8,128]{2,1,0:T(8,128)S(1)}, f32[3,8,128]{2,1,0:T(8,128)S(1)}, u32[]{:S(2)}, u32[]{:S(2)}) collective-permute-start(f32[3,8,128]{2,1,0:T(8,128)S(1)} %get-tuple-element.8), channel_id=1, source_target_pairs={{0,1},{1,0},{2,3},{3,2},{4,5},{5,4},{6,7},{7,6},{8,9},{9,8},{10,11... | collective-permute-start | bytes 36872 | tf_op jit(solution)/shard_map/ppermute | solution.py:363
  4.3 2.0 %collective-permute-start.1 = (f32[3,8,128]{2,1,0:T(8,128)S(1)}, f32[3,8,128]{2,1,0:T(8,128)S(1)}, u32[]{:S(2)}, u32[]{:S(2)}) collective-permute-start(f32[3,8,128]{2,1,0:T(8,128)S(1)} %get-tuple-element.9), channel_id=1, source_target_pairs={{0,7},{1,2},{2,1},{3,4},{4,3},{5,6},{6,5},{7,0},{8,15},{9,10},{10,... | collective-permute-start | bytes 36872 | tf_op jit(solution)/shard_map/ppermute | solution.py:363
  6.3 1.0 %collective-permute-done.got0 = f32[3,8,128]{2,1,0:T(8,128)S(1)} collective-permute-done((f32[3,8,128]{2,1,0:T(8,128)S(1)}, f32[3,8,128]{2,1,0:T(8,128)S(1)}, u32[]{:S(2)}, u32[]{:S(2)}) %collective-permute-start) | collective-permute-done | bytes 12320 | tf_op jit(solution)/shard_map/ppermute | solution.py:363
  7.3 2.9 %collective-permute-done.1.got1 = f32[3,8,128]{2,1,0:T(8,128)S(1)} collective-permute-done((f32[3,8,128]{2,1,0:T(8,128)S(1)}, f32[3,8,128]{2,1,0:T(8,128)S(1)}, u32[]{:S(2)}, u32[]{:S(2)}) %collective-permute-start.1) | collective-permute-done | bytes 12320 | tf_op jit(solution)/shard_map/ppermute | solution.py:363
  10.1 0.0 copy-done.4
  10.1 5.4 %first.3 = (f32[19,9,32,128]{3,2,1,0:T(8,128)}, f32[24,9,8,128]{3,2,1,0:T(8,128)S(1)}, f32[24,9,4,128]{3,2,1,0:T(4,128)S(1)}, f32[24,9,4,128]{3,2,1,0:T(4,128)S(1)}) custom-call(f32[3]{0:T(128)S(1)} %copy-done.4, f32[19,4,8,1024]{3,2,1,0:T(8,128)S(1)} %copy-done, s32[4,8,1024]{2,1,0:T(8,128)S(1)} %copy-done.2, f32[3,8,128]{2,1,0:T(8,128)S(1)} %collective-permute-done.got0, ...), custom_call_target="tpu_custom_call" | custom-call | tf_op jit(solution)/shard_map/first/pallas_call | solution.py:386
  15.5 0.0 collective-permute-start.2
  15.5 8.4 %collective-permute-start.3 = (f32[24,9,4,128]{3,2,1,0:T(4,128)S(1)}, f32[24,9,4,128]{3,2,1,0:T(4,128)S(1)}, u32[]{:S(2)}, u32[]{:S(2)}) collective-permute-start(f32[24,9,4,128]{3,2,1,0:T(4,128)S(1)} %get-tuple-element.13), channel_id=1, source_target_pairs={{0,248},{8,16},{16,8},{24,32},{32,24},{40,48},{48,40},{56,64},{64,... | collective-permute-start | bytes 1327112 | tf_op jit(solution)/shard_map/ppermute | solution.py:363
  24.0 0.0 collective-permute-done.2.near
  24.0 6.0 %collective-permute-done.3.far = f32[24,9,4,128]{3,2,1,0:T(4,128)S(1)} collective-permute-done((f32[24,9,4,128]{3,2,1,0:T(4,128)S(1)}, f32[24,9,4,128]{3,2,1,0:T(4,128)S(1)}, u32[]{:S(2)}, u32[]{:S(2)}) %collective-permute-start.3) | collective-permute-done | bytes 442400 | tf_op jit(solution)/shard_map/ppermute | solution.py:363
  30.0 0.0 copy-done.3
  30.0 0.0 copy-start.1
  30.0 1.8 %copy-done.1 = f32[19,9,32,128]{3,2,1,0:T(8,128)S(1)} copy-done((f32[19,9,32,128]{3,2,1,0:T(8,128)S(1)}, f32[19,9,32,128]{3,2,1,0:T(8,128)}, u32[]{:S(2)}) %copy-start.1) | copy-done | bytes 2801688
  31.8 6.1 %last.3 = (f32[4,8,1024]{2,1,0:T(8,128)}, f32[3,4,8,1024]{3,2,1,0:T(8,128)}) custom-call(f32[3]{0:T(128)S(1)} %copy-done.4, f32[19,9,32,128]{3,2,1,0:T(8,128)S(1)} %copy-done.1, f32[24,9,8,128]{3,2,1,0:T(8,128)S(1)} %get-tuple-element.11.edge, f32[24,9,4,128]{3,2,1,0:T(4,128)S(1)} %collective-permute-done.2.near, ...), custom_call_target="tpu_custom_call" | custom-call | tf_op jit(solution)/shard_map/last/pallas_call | solution.py:401
Async XLA Ops:
  0.6 1.7 %copy-start = (f32[19,4,8,1024]{3,2,1,0:T(8,128)S(1)}, f32[19,4,8,1024]{3,2,1,0:T(8,128)}, u32[]{:S(2)}) copy-start(f32[19,4,8,1024]{3,2,1,0:T(8,128)} %pop.1) | copy-start | bytes 7471108
  2.3 0.9 %copy-start.2 = (s32[4,8,1024]{2,1,0:T(8,128)S(1)}, s32[4,8,1024]{2,1,0:T(8,128)}, u32[]{:S(2)}) copy-start(s32[4,8,1024]{2,1,0:T(8,128)} %mask.3) | copy-start | bytes 393220
  3.2 6.9 %copy-start.4 = (f32[3]{0:T(128)S(1)}, f32[3]{0:T(128)}, u32[]{:S(2)}) copy-start(f32[3]{0:T(128)} %force_ref.3) | copy-start | bytes 40
  3.2 26.7 %copy-start.3 = (s32[4,8,1024]{2,1,0:T(8,128)S(1)}, s32[4,8,1024]{2,1,0:T(8,128)}, u32[]{:S(2)}) copy-start(s32[4,8,1024]{2,1,0:T(8,128)} %mask.3) | copy-start | bytes 393220
  3.5 3.8 %collective-permute-start = (f32[3,8,128]{2,1,0:T(8,128)S(1)}, f32[3,8,128]{2,1,0:T(8,128)S(1)}, u32[]{:S(2)}, u32[]{:S(2)}) collective-permute-start(f32[3,8,128]{2,1,0:T(8,128)S(1)} %get-tuple-element.8), channel_id=1, source_target_pairs={{0,1},{1,0},{2,3},{3,2},{4,5},{5,4},{6,7},{7,6},{8,9},{9,8},{10,11... | collective-permute-start | bytes 36872 | tf_op jit(solution)/shard_map/ppermute | solution.py:363
  4.3 5.8 %collective-permute-start.1 = (f32[3,8,128]{2,1,0:T(8,128)S(1)}, f32[3,8,128]{2,1,0:T(8,128)S(1)}, u32[]{:S(2)}, u32[]{:S(2)}) collective-permute-start(f32[3,8,128]{2,1,0:T(8,128)S(1)} %get-tuple-element.9), channel_id=1, source_target_pairs={{0,7},{1,2},{2,1},{3,4},{4,3},{5,6},{6,5},{7,0},{8,15},{9,10},{10,... | collective-permute-start | bytes 36872 | tf_op jit(solution)/shard_map/ppermute | solution.py:363
  15.5 8.4 %collective-permute-start.2 = (f32[24,9,4,128]{3,2,1,0:T(4,128)S(1)}, f32[24,9,4,128]{3,2,1,0:T(4,128)S(1)}, u32[]{:S(2)}, u32[]{:S(2)}) collective-permute-start(f32[24,9,4,128]{3,2,1,0:T(4,128)S(1)} %get-tuple-element.12), channel_id=1, source_target_pairs={{0,8},{8,0},{16,24},{24,16},{32,40},{40,32},{48,56},{56,48},{64,72... | collective-permute-start | bytes 1327112 | tf_op jit(solution)/shard_map/ppermute | solution.py:363
  15.5 14.4 %collective-permute-start.3 = (f32[24,9,4,128]{3,2,1,0:T(4,128)S(1)}, f32[24,9,4,128]{3,2,1,0:T(4,128)S(1)}, u32[]{:S(2)}, u32[]{:S(2)}) collective-permute-start(f32[24,9,4,128]{3,2,1,0:T(4,128)S(1)} %get-tuple-element.13), channel_id=1, source_target_pairs={{0,248},{8,16},{16,8},{24,32},{32,24},{40,48},{48,40},{56,64},{64,... | collective-permute-start | bytes 1327112 | tf_op jit(solution)/shard_map/ppermute | solution.py:363
  30.0 1.8 %copy-start.1 = (f32[19,9,32,128]{3,2,1,0:T(8,128)S(1)}, f32[19,9,32,128]{3,2,1,0:T(8,128)}, u32[]{:S(2)}) copy-start(f32[19,9,32,128]{3,2,1,0:T(8,128)} %get-tuple-element.10.r2_hbm) | copy-start | bytes 8404996
where the time goes:
time: 38 us; the launch traced here: 37.9 us
  Pallas kernels  11.8 us (31%)
  starting transfers between devices  11.2 us (29%)
  waiting for transfers between devices  9.81 us (26%)
  local copies, waits for them, and re-layouts  4.4 us (12%)
  between operations  0.66 us (2%)
    ppermute x4, starting transfers between devices, swap(): return lax.ppermute(x, axis, pairs)  11.2 us
    ppermute x4, waiting for transfers between devices, swap(): return lax.ppermute(x, axis, pairs)  9.81 us
    pallas_call x1, Pallas kernels, local(): pl.pallas_call(last_kernel, out_shape=(sds(4, 8, 1024), sds(3, 4, 8, 1024...  6.12 us
    pallas_call x1, Pallas kernels, local(): pl.pallas_call(first_kernel, out_shape=(sds(19, 9, 32, 128), sds(NMSG, 9,...  5.43 us
    unnamed x10, local copies, waits for them, and re-layouts  4.4 us
  transfers between devices with their start and end apart: 4, of which 3 were waited for; matrix products, arithmetic and copies ran while one was open for 0% of the time, Pallas kernels for 0%

commit v1 on v0

--- a/solution.py
+++ b/solution.py
@@ -111,29 +111,39 @@
     return out
 
 
-def along_z(get, t, cz, lane):
-    cur = get(t)
+def along_z(get, t, cz, lane, split=False):
+    def at(s):
+        return get(None if split and s == 8 else s)
+
+    if isinstance(t, int):
+        prev, succ = (t + 8) % 9, (t + 1) % 9
+    elif split:
+        prev, succ = t - 1, t + 1
+    else:
+        prev, succ = jnp.where(t == 0, 8, t - 1), jnp.where(t == 8, 0, t + 1)
+    cur = at(t) if isinstance(t, int) else get(t)
     if cz == 0:
         return cur
     if cz == 1:
-        before = get(jnp.where(t == 0, 8, t - 1))
+        before = at(prev) if isinstance(t, int) else get(prev)
         return pltpu.roll(jnp.where(lane == 127, before, cur), 1, axis=1)
-    after = get(jnp.where(t == 8, 0, t + 1))
+    after = at(succ) if isinstance(t, int) else get(succ)
     return pltpu.roll(jnp.where(lane == 0, after, cur), 127, axis=1)
 
 
-def stream_own(ref, halo, p, t, lane, row):
+def stream_own(load, halo, p, t, lane, row):
+    split = halo is None
     f = []
     for k in range(19):
         cx, cy, cz = VEL[k]
-        own = ref[OPP[k], t, 8 * p : 8 * p + 8, :]
+        own = load(OPP[k], None if split and isinstance(t, int) and t == 8 else t, p)
         q = p - cx
         if k == 0 or q < 0 or q > 3:
             f.append(own)
             continue
 
         def get(s, k=k, q=q, cy=cy):
-            v = ref[k, s, 8 * q : 8 * q + 8, :]
+            v = load(k, s, q)
             if cy == 0 or halo is None:
                 return v
             if cy == 1:
@@ -143,7 +153,7 @@
             rim = jnp.broadcast_to(halo[i, s, sub : sub + 1, :], (8, 128))
             return jnp.where(row == at, rim, v)
 
-        v = along_z(get, t, cz, lane)
+        v = along_z(get, t, cz, lane, split)
         if cy == 1:
             v = pltpu.roll(v, 1, axis=0)
         elif cy == -1:
@@ -162,9 +172,9 @@
     return jnp.where(v < BIG, v, own)
 
 
-def edges(ref, k, t, lower, upper):
-    a = ref[k, t, pl.ds(lower, 4, stride=8), :]
-    b = ref[FLIP[k], t, pl.ds(upper, 4, stride=8), :]
+def edges(ref, flipped, lower, upper):
+    a = ref[pl.ds(lower, 4, stride=8), :]
+    b = flipped[pl.ds(upper, 4, stride=8), :]
     return jnp.concatenate([a, b], axis=0)
 
 
@@ -177,7 +187,25 @@
     return fx, jnp.where(row < 4, fy, -fy), fz
 
 
-def pack_kernel(first, last, mask_first, mask_last, out0, out1):
+GROUPS = ((0, 5), (5, 10), (10, 15), (15, 19))
+
+
+def pack_kernel(pop_hbm, mask_hbm, out1, out0, first, last, mask_first, mask_last, sem):
+    copies = [
+        pltpu.make_async_copy(mask_hbm.at[:, :, 0:128], mask_first, sem.at[0]),
+        pltpu.make_async_copy(mask_hbm.at[:, :, 896:1024], mask_last, sem.at[1]),
+    ]
+    for i, (a, b) in enumerate(GROUPS):
+        for j, (at, to) in enumerate(((0, first), (896, last))):
+            copies.append(
+                pltpu.make_async_copy(
+                    pop_hbm.at[a:b, :, :, at : at + 128], to.at[a:b], sem.at[2 + 2 * i + j]
+                )
+            )
+    for copy in copies:
+        copy.start()
+    for copy in copies:
+        copy.wait()
     lane = lanes()
     even = lax.rem(lax.axis_index("gz"), 2) == 0
     group = lane // 4
@@ -203,9 +231,58 @@
         out1[tile] = jnp.where(even, left, right)
 
 
-def first_kernel(force_ref, pop, mask, got0, got1, r2, edge, near, far, r1, f1, rim):
+def rim_values(e1, e2, e3, t, force_rim, lane, row):
+    own = [e1(k, t) for k in range(19)]
+    values = [own[k] for k in OUT]
+    for k in LOCAL:
+        if k == 0:
+            values.append(own[0])
+        else:
+            src = e1 if k in FLAT else e2
+            values.append(stream_rim(lambda s, k=k, src=src: src(k, s), own[OPP[k]], k, t, lane, row))
+    own = [e2(k, t) for k in range(19)]
+    f = [own[0]]
+    for k in range(1, 19):
+        src = e2 if k in FLAT else (e1 if k in IN else e3)
+        f.append(stream_rim(lambda s, k=k, src=src: src(k, s), own[OPP[k]], k, t, lane, row))
+    g = collide(f, force_rim)
+    return values + [g[k] for k in OUT]
+
+
+def collide_kernel(force_ref, pop, mask, r1, e1, e2, e3, inner):
     lane, row = lanes(), rows()
     force = force_of(force_ref)
+    force_rim = rim_force(force, row)
+
+    @pl.loop(0, 8)
+    def _(t):
+        at = pl.ds(pl.multiple_of(t * 128, 128), 128)
+        for p in range(4):
+            f = [pop[k, p, :, at] for k in range(19)]
+            f[0] = jnp.where(mask[p, :, at] > 0, NAN, f[0])
+            g = collide(f, force)
+            for k in range(19):
+                r1[k, t, 8 * p : 8 * p + 8, :] = g[k]
+        for k in range(19):
+            e1[t, k] = edges(r1.at[k, t], r1.at[FLIP[k], t], 0, 7)
+            e2[t, k] = edges(r1.at[k, t], r1.at[FLIP[k], t], 1, 6)
+        for i, k in enumerate(OUT):
+            e3[t, i] = edges(r1.at[k, t], r1.at[FLIP[k], t], 2, 5)
+
+    @pl.loop(1, 7)
+    def _(t):
+        values = rim_values(
+            lambda k, s: e1[s, k], lambda k, s: e2[s, k], lambda k, s: e3[s, OUT.index(k)],
+            t, force_rim, lane, row,
+        )
+        for i, v in enumerate(values):
+            inner[t - 1, i] = v
+
+
+def rim_kernel(force_ref, e1, e2, e3, inner, got1, got0, r1h, edge, far, near, strip, h1, h2, h3):
+    lane, row = lanes(), rows()
+    force = force_of(force_ref)
+    force_rim = rim_force(force, row)
     even_z = lax.rem(lax.axis_index("gz"), 2) == 0
     even_y = lax.rem(lax.axis_index("gy"), 2) == 0
     for tile in range(3):
@@ -219,51 +296,79 @@
             k, p = i // 4, i % 4
             x = pltpu.roll(from_right, 128 - 4 * s, axis=1) if s else from_right
             y = pltpu.roll(from_left, 124 - 4 * s, axis=1) if s != 31 else from_left
-            rim[k, p] = jnp.where(lane < 64, x, y)
-
-    def put(t, p, f):
-        g = collide(f, force)
+            strip[k, p] = jnp.where(lane < 64, x, y)
+    for p in range(4):
+        g = collide([strip[k, p] for k in range(19)], force)
         for k in range(19):
-            r1[k, t, 8 * p : 8 * p + 8, :] = g[k]
-
-    @pl.loop(0, 8)
-    def _(t):
-        at = pl.ds(pl.multiple_of(t * 128, 128), 128)
+            r1h[k, 8 * p : 8 * p + 8, :] = g[k]
+    for k in range(19):
+        h1[k] = edges(r1h.at[k], r1h.at[FLIP[k]], 0, 7)
+        h2[k] = edges(r1h.at[k], r1h.at[FLIP[k]], 1, 6)
+    for i, k in enumerate(OUT):
+        h3[i] = edges(r1h.at[k], r1h.at[FLIP[k]], 2, 5)
+
+    def put(t, i, v):
+        edge[i, t] = v
+        w = jnp.where(even_y, pltpu.roll(v, 4, axis=0), v)
+        near[i, t] = w[0:4]
+        far[i, t] = w[4:8]
+
+    for t in (0, 7, 8):
+        values = rim_values(
+            lambda k, s: h1[k] if s == 8 else e1[s, k],
+            lambda k, s: h2[k] if s == 8 else e2[s, k],
+            lambda k, s: h3[OUT.index(k)] if s == 8 else e3[s, OUT.index(k)],
+            t, force_rim, lane, row,
+        )
+        for i, v in enumerate(values):
+            put(t, i, v)
+
+    @pl.loop(1, 7)
+    def _(t):
+        for i in range(NMSG):
+            put(t, i, inner[t - 1, i])
+
+
+def middle_kernel(force_ref, r1, r1h, r2_hbm, r2, sem):
+    lane, row = lanes(), rows()
+    force = force_of(force_ref)
+
+    def copy(t):
+        return pltpu.make_async_copy(r2.at[t], r2_hbm.at[t], sem.at[t])
+
+    def step(t):
+        def get(k, s, p):
+            return r1h[k, 8 * p : 8 * p + 8, :] if s is None else r1[k, s, 8 * p : 8 * p + 8, :]
+
         for p in range(4):
-            f = [pop[k, p, :, at] for k in range(19)]
-            f[0] = jnp.where(mask[p, :, at] > 0, NAN, f[0])
-            put(t, p, f)
-
-    for p in range(4):
-        put(8, p, [rim[k, p] for k in range(19)])
-
-    @pl.loop(0, 9)
-    def _(t):
-        for p in range(4):
-            f = stream_own(r1, None, p, t, lane, row)
+            g = collide(stream_own(get, None, p, t, lane, row), force)
             for k in range(19):
-                f1[k, t, 8 * p : 8 * p + 8, :] = f[k]
-            g = collide(f, force)
-            for k in range(19):
-                r2[k, t, 8 * p : 8 * p + 8, :] = g[k]
-
-    @pl.loop(0, 9)
-    def _(t):
-        values = [edges(r1, k, t, 0, 7) for k in OUT]
-        values += [edges(f1, k, t, 0, 7) for k in LOCAL]
-        values += [edges(r2, k, t, 1, 6) for k in OUT]
-        for i, v in enumerate(values):
-            edge[i, t] = v
-            w = jnp.where(even_y, pltpu.roll(v, 4, axis=0), v)
-            near[i, t] = w[0:4]
-            far[i, t] = w[4:8]
+                r2[t, k, 8 * p : 8 * p + 8, :] = g[k]
+        copy(t).start()
+
+    for t in (0, 7, 8):
+        step(t)
+
+    @pl.loop(1, 7)
+    def _(t):
+        step(t)
+
+    for t in range(9):
+        copy(t).wait()
 
 
 def last_kernel(
-    force_ref, r2_hbm, edge, near, far, mask, density, velocity, r2, r3, got, r2h, r2e, r3h, sem
+    force_ref, r2_hbm, edge, far, near, mask, density, velocity, r2, r3, got, r2h, r2e, r3h, sem
 ):
     copy = pltpu.make_async_copy(r2_hbm, r2, sem)
     copy.start()
+
+    def load2(k, s, p):
+        return r2[s, k, 8 * p : 8 * p + 8, :]
+
+    def load3(k, s, p):
+        return r3[s, k, 8 * p : 8 * p + 8, :]
+
     lane, row = lanes(), rows()
     force = force_of(force_ref)
     force_rim = rim_force(force, row)
@@ -287,8 +392,8 @@
             f[k] = stream_rim(lambda s, i=i: got[i, s], own, k, t, lane, row)
         g = collide(f, force_rim)
         for k in range(19):
-            r2[k, t, pl.ds(0, 4, stride=8), :] = g[k][0:4]
-            r2[FLIP[k], t, pl.ds(7, 4, stride=8), :] = g[k][4:8]
+            r2[t, k, pl.ds(0, 4, stride=8), :] = g[k][0:4]
+            r2[t, FLIP[k], pl.ds(7, 4, stride=8), :] = g[k][4:8]
         for i, k in enumerate(OUT):
             r2e[i, t] = g[k]
         f = [None] * 19
@@ -320,15 +425,15 @@
         for i, k in enumerate(IN):
             r3h[i, t] = g[k]
         for p in range(4):
-            g = collide(stream_own(r2, r2h, p, t, lane, row), force)
+            g = collide(stream_own(load2, r2h, p, t, lane, row), force)
             for k in range(19):
-                r3[k, t, 8 * p : 8 * p + 8, :] = g[k]
+                r3[t, k, 8 * p : 8 * p + 8, :] = g[k]
 
     @pl.loop(0, 8)
     def _(t):
         at = pl.ds(pl.multiple_of(t * 128, 128), 128)
         for p in range(4):
-            f = stream_own(r3, r3h, p, t, lane, row)
+            f = stream_own(load3, r3h, p, t, lane, row)
             rho = f[0]
             for k in range(1, 19):
                 rho = rho + f[k]
@@ -346,15 +451,30 @@
 
 VMEM = pl.BlockSpec(memory_space=pltpu.VMEM)
 SMEM = pl.BlockSpec(memory_space=pltpu.SMEM)
-ANY = pl.BlockSpec(memory_space=pl.ANY)
-
-
-def params():
-    return pltpu.CompilerParams(vmem_limit_bytes=48 * 1024 * 1024)
+HBM = pl.BlockSpec(memory_space=pltpu.HBM)
+
+
+def call(kernel, name, us, out_shape, in_specs, out_specs, scratch, room=40):
+    return pl.pallas_call(
+        kernel,
+        out_shape=out_shape,
+        in_specs=in_specs,
+        out_specs=out_specs,
+        scratch_shapes=scratch,
+        compiler_params=pltpu.CompilerParams(vmem_limit_bytes=room * 1024 * 1024),
+        cost_estimate=pl.CostEstimate(
+            flops=int(us * 1e6), bytes_accessed=int(us * 3e6), transcendentals=0
+        ),
+        name=name,
+    )
 
 
 def sds(*shape):
     return jax.ShapeDtypeStruct(shape, F32)
+
+
+def buf(*shape):
+    return pltpu.VMEM(shape, F32)
 
 
 def swap(x, axis, parity):
@@ -364,57 +484,41 @@
 
 
 def local(pop, mask, force):
-    z0, z1 = pl.pallas_call(
-        pack_kernel,
-        out_shape=(sds(3, 8, 128), sds(3, 8, 128)),
-        grid=(1,),
-        in_specs=[
-            pl.BlockSpec((19, 4, 8, 128), lambda i: (0, 0, 0, 0)),
-            pl.BlockSpec((19, 4, 8, 128), lambda i: (0, 0, 0, 7)),
-            pl.BlockSpec((4, 8, 128), lambda i: (0, 0, 0)),
-            pl.BlockSpec((4, 8, 128), lambda i: (0, 0, 7)),
-        ],
-        out_specs=(
-            pl.BlockSpec((3, 8, 128), lambda i: (0, 0, 0)),
-            pl.BlockSpec((3, 8, 128), lambda i: (0, 0, 0)),
-        ),
-        compiler_params=params(),
-        name="pack",
-    )(pop, pop, mask, mask)
+    far_memory = [pltpu.with_memory_space_constraint(x, pltpu.HBM) for x in (pop, mask)]
+    z1, z0 = call(
+        pack_kernel, "pack", 0.7,
+        (sds(3, 8, 128), sds(3, 8, 128)), [HBM, HBM], (VMEM, VMEM),
+        [buf(19, 4, 8, 128), buf(19, 4, 8, 128), pltpu.VMEM((4, 8, 128), jnp.int32),
+         pltpu.VMEM((4, 8, 128), jnp.int32), pltpu.SemaphoreType.DMA((10,))],
+    )(*far_memory)
+    got1 = swap(z1, "gz", 1)
     got0 = swap(z0, "gz", 0)
-    got1 = swap(z1, "gz", 1)
-    r2, edge, near, far = pl.pallas_call(
-        first_kernel,
-        out_shape=(sds(19, 9, 32, 128), sds(NMSG, 9, 8, 128), sds(NMSG, 9, 4, 128), sds(NMSG, 9, 4, 128)),
-        in_specs=[SMEM, VMEM, VMEM, VMEM, VMEM],
-        out_specs=(VMEM, VMEM, VMEM, VMEM),
-        scratch_shapes=[
-            pltpu.VMEM((19, 9, 32, 128), F32),
-            pltpu.VMEM((19, 9, 32, 128), F32),
-            pltpu.VMEM((19, 4, 8, 128), F32),
-        ],
-        compiler_params=params(),
-        name="first",
-    )(force, pop, mask, got0, got1)
+    r1, e1, e2, e3, inner = call(
+        collide_kernel, "collide", 3.0,
+        (sds(19, 8, 32, 128), sds(8, 19, 8, 128), sds(8, 19, 8, 128), sds(8, 5, 8, 128),
+         sds(6, NMSG, 8, 128)),
+        [SMEM, VMEM, VMEM], (VMEM,) * 5, [],
+    )(force, pop, mask)
+    r1h, edge, far, near = call(
+        rim_kernel, "rim", 1.0,
+        (sds(19, 32, 128), sds(NMSG, 9, 8, 128), sds(NMSG, 9, 4, 128), sds(NMSG, 9, 4, 128)),
+        [SMEM] + [VMEM] * 6, (VMEM,) * 4,
+        [buf(19, 4, 8, 128), buf(19, 8, 128), buf(19, 8, 128), buf(5, 8, 128)],
+    )(force, e1, e2, e3, inner, got1, got0)
     far = swap(far, "gy", 1)
     near = swap(near, "gy", 0)
-    return pl.pallas_call(
-        last_kernel,
-        out_shape=(sds(4, 8, 1024), sds(3, 4, 8, 1024)),
-        in_specs=[SMEM, ANY, VMEM, VMEM, VMEM, VMEM],
-        out_specs=(VMEM, VMEM),
-        scratch_shapes=[
-            pltpu.VMEM((19, 9, 32, 128), F32),
-            pltpu.VMEM((19, 9, 32, 128), F32),
-            pltpu.VMEM((NMSG, 9, 8, 128), F32),
-            pltpu.VMEM((19, 9, 8, 128), F32),
-            pltpu.VMEM((5, 9, 8, 128), F32),
-            pltpu.VMEM((5, 9, 8, 128), F32),
-            pltpu.SemaphoreType.DMA,
-        ],
-        compiler_params=params(),
-        name="last",
-    )(force, r2, edge, near, far, mask)
+    r2 = call(
+        middle_kernel, "middle", 3.0,
+        sds(9, 19, 32, 128), [SMEM, VMEM, VMEM], HBM,
+        [buf(9, 19, 32, 128), pltpu.SemaphoreType.DMA((9,))],
+    )(force, r1, r1h)
+    return call(
+        last_kernel, "last", 5.0,
+        (sds(4, 8, 1024), sds(3, 4, 8, 1024)),
+        [SMEM, HBM, VMEM, VMEM, VMEM, VMEM], (VMEM, VMEM),
+        [buf(9, 19, 32, 128), buf(9, 19, 32, 128), buf(NMSG, 9, 8, 128), buf(19, 9, 8, 128),
+         buf(5, 9, 8, 128), buf(5, 9, 8, 128), pltpu.SemaphoreType.DMA],
+    )(force, r2, edge, far, near, mask)
 
 
 def solution(mesh):

time: 38 us -> 29.6 us (0.78)
  the two profiles are of different devices: /device:TPU:24 before, /device:TPU:8 now
where the time goes in v1:
time: 29.6 us; the launch traced here: 29.5 us
  Pallas kernels  14.4 us (49%)
  starting transfers between devices  11.5 us (39%)
  waiting for transfers between devices  2.9 us (10%)
  between operations  0.7 us (2%)
    ppermute x4, starting transfers between devices, swap(): return lax.ppermute(x, axis, pairs)  11.5 us
    pallas_call x1, Pallas kernels, local(): call(last_kernel, 'last', 5.0, (sds(4, 8, 1024), sds(3, 4, 8, 1024)), [SM...  6.11 us
    pallas_call x1, Pallas kernels, local(): call(middle_kernel, 'middle', 3.0, sds(9, 19, 32, 128), [SMEM, VMEM, VMEM...  3.08 us
    ppermute x4, waiting for transfers between devices, swap(): return lax.ppermute(x, axis, pairs)  2.9 us
    pallas_call x1, Pallas kernels, local(): call(collide_kernel, 'collide', 3.0, (sds(19, 8, 32, 128), sds(8, 19, 8,...  2.51 us
    pallas_call x1, Pallas kernels, local(): call(pack_kernel, 'pack', 0.7, (sds(3, 8, 128), sds(3, 8, 128)), [HBM, HB...  1.6 us
    pallas_call x1, Pallas kernels, local(): call(rim_kernel, 'rim', 1.0, (sds(19, 32, 128), sds(NMSG, 9, 8, 128), sds...  1.15 us
  transfers between devices with their start and end apart: 4, of which 1 were waited for; matrix products, arithmetic and copies ran while one was open for 0% of the time, Pallas kernels for 19%

profile of v1, /device:TPU:8, one launch (start us, length us, event | category | flops | bytes accessed | tf_op | source)
XLA Modules:
  0.0 29.5 jit_solution(10249675506419056343)
XLA Ops:
  0.6 0.0 copy-start.1
  0.6 0.0 copy-start
  0.6 0.0 copy-start.2
  0.7 1.6 %pack.1 = (f32[3,8,128]{2,1,0:T(8,128)S(1)}, f32[3,8,128]{2,1,0:T(8,128)S(1)}) custom-call(f32[19,4,8,1024]{3,2,1,0:T(8,128)} %pop_hbm.1, s32[4,8,1024]{2,1,0:T(8,128)} %mask.3), custom_call_target="tpu_custom_call" | custom-call | flops 700000 | bytes 2100000 | tf_op jit(solution)/shard_map/pack/pallas_call | solution.py:488
  2.3 1.7 %collective-permute-start = (f32[3,8,128]{2,1,0:T(8,128)S(1)}, f32[3,8,128]{2,1,0:T(8,128)S(1)}, u32[]{:S(2)}, u32[]{:S(2)}) collective-permute-start(f32[3,8,128]{2,1,0:T(8,128)S(1)} %get-tuple-element.18), channel_id=1, source_target_pairs={{0,7},{1,2},{2,1},{3,4},{4,3},{5,6},{6,5},{7,0},{8,15},{9,10},{10,... | collective-permute-start | bytes 36872 | tf_op jit(solution)/shard_map/ppermute | solution.py:483
  3.9 2.8 %collective-permute-start.1 = (f32[3,8,128]{2,1,0:T(8,128)S(1)}, f32[3,8,128]{2,1,0:T(8,128)S(1)}, u32[]{:S(2)}, u32[]{:S(2)}) collective-permute-start(f32[3,8,128]{2,1,0:T(8,128)S(1)} %get-tuple-element.19), channel_id=1, source_target_pairs={{0,1},{1,0},{2,3},{3,2},{4,5},{5,4},{6,7},{7,6},{8,9},{9,8},{10,11... | collective-permute-start | bytes 36872 | tf_op jit(solution)/shard_map/ppermute | solution.py:483
  6.7 0.0 copy-done.1
  6.7 0.0 copy-done
  6.8 0.0 copy-done.2
  6.8 2.5 %collide.1 = (f32[19,8,32,128]{3,2,1,0:T(8,128)S(1)}, f32[8,19,8,128]{3,2,1,0:T(8,128)S(1)}, f32[8,19,8,128]{3,2,1,0:T(8,128)S(1)}, f32[8,5,8,128]{3,2,1,0:T(8,128)S(1)}, f32[6,24,8,128]{3,2,1,0:T(8,128)S(1)}) custom-call(f32[3]{0:T(128)S(1)} %copy-done.2, f32[19,4,8,1024]{3,2,1,0:T(8,128)S(1)} %copy-done, s32[4,8,1024]{2,1,0:T(8,128)S(1)} %copy-done.1), custom_call_target="tpu_custom_call" | custom-call | flops 3000000 | bytes 9000000 | tf_op jit(solution)/shard_map/collide/pallas_call | solution.py:496
  9.3 0.0 collective-permute-done.got1
  9.3 0.0 collective-permute-done.1.got0
  9.3 1.2 %rim.1 = (f32[19,32,128]{2,1,0:T(8,128)S(1)}, f32[24,9,8,128]{3,2,1,0:T(8,128)S(1)}, f32[24,9,4,128]{3,2,1,0:T(4,128)S(1)}, f32[24,9,4,128]{3,2,1,0:T(4,128)S(1)}) custom-call(f32[3]{0:T(128)S(1)} %copy-done.2, f32[8,19,8,128]{3,2,1,0:T(8,128)S(1)} %get-tuple-element.14.e1, f32[8,19,8,128]{3,2,1,0:T(8,128)S(1)} %get-tuple-element.15.e2, ...), custom_call_target="tpu_custom_call" | custom-call | flops 1000000 | bytes 3000000 | tf_op jit(solution)/shard_map/rim/pallas_call | solution.py:502
  10.4 7.0 %collective-permute-start.2 = (f32[24,9,4,128]{3,2,1,0:T(4,128)S(1)}, f32[24,9,4,128]{3,2,1,0:T(4,128)S(1)}, u32[]{:S(2)}, u32[]{:S(2)}) collective-permute-start(f32[24,9,4,128]{3,2,1,0:T(4,128)S(1)} %get-tuple-element.22), channel_id=1, source_target_pairs={{0,248},{8,16},{16,8},{24,32},{32,24},{40,48},{48,40},{56,64},{64,... | collective-permute-start | bytes 1327112 | tf_op jit(solution)/shard_map/ppermute | solution.py:483
  17.4 0.0 collective-permute-start.3
  17.4 3.1 %middle.1.r2_hbm = f32[9,19,32,128]{3,2,1,0:T(8,128)S(1)} custom-call(f32[3]{0:T(128)S(1)} %copy-done.2, f32[19,8,32,128]{3,2,1,0:T(8,128)S(1)} %get-tuple-element.13.r1, f32[19,32,128]{2,1,0:T(8,128)S(1)} %get-tuple-element.20.r1h), custom_call_target="tpu_custom_call" | custom-call | flops 3000000 | bytes 9000000 | tf_op jit(solution)/shard_map/middle/pallas_call | solution.py:510
  20.5 2.9 %collective-permute-done.2.far = f32[24,9,4,128]{3,2,1,0:T(4,128)S(1)} collective-permute-done((f32[24,9,4,128]{3,2,1,0:T(4,128)S(1)}, f32[24,9,4,128]{3,2,1,0:T(4,128)S(1)}, u32[]{:S(2)}, u32[]{:S(2)}) %collective-permute-start.2) | collective-permute-done | bytes 442400 | tf_op jit(solution)/shard_map/ppermute | solution.py:483
  23.4 0.0 collective-permute-done.3.near
  23.4 6.1 %last.1 = (f32[4,8,1024]{2,1,0:T(8,128)}, f32[3,4,8,1024]{3,2,1,0:T(8,128)}) custom-call(f32[3]{0:T(128)S(1)} %copy-done.2, f32[9,19,32,128]{3,2,1,0:T(8,128)S(1)} %middle.1.r2_hbm, f32[24,9,8,128]{3,2,1,0:T(8,128)S(1)} %get-tuple-element.21.edge, f32[24,9,4,128]{3,2,1,0:T(4,128)S(1)} %collective-permute-done.2.far, ...), custom_call_target="tpu_custom_call" | custom-call | flops 5000000 | bytes 15000000 | tf_op jit(solution)/shard_map/last/pallas_call | solution.py:515
Async XLA Ops:
  0.6 6.1 %copy-start.1 = (s32[4,8,1024]{2,1,0:T(8,128)S(1)}, s32[4,8,1024]{2,1,0:T(8,128)}, u32[]{:S(2)}) copy-start(s32[4,8,1024]{2,1,0:T(8,128)} %mask.3) | copy-start | bytes 393220
  0.6 6.1 %copy-start = (f32[19,4,8,1024]{3,2,1,0:T(8,128)S(1)}, f32[19,4,8,1024]{3,2,1,0:T(8,128)}, u32[]{:S(2)}) copy-start(f32[19,4,8,1024]{3,2,1,0:T(8,128)} %pop_hbm.1) | copy-start | bytes 7471108
  0.6 6.1 %copy-start.2 = (f32[3]{0:T(128)S(1)}, f32[3]{0:T(128)}, u32[]{:S(2)}) copy-start(f32[3]{0:T(128)} %force_ref.7) | copy-start | bytes 40
  2.3 7.0 %collective-permute-start = (f32[3,8,128]{2,1,0:T(8,128)S(1)}, f32[3,8,128]{2,1,0:T(8,128)S(1)}, u32[]{:S(2)}, u32[]{:S(2)}) collective-permute-start(f32[3,8,128]{2,1,0:T(8,128)S(1)} %get-tuple-element.18), channel_id=1, source_target_pairs={{0,7},{1,2},{2,1},{3,4},{4,3},{5,6},{6,5},{7,0},{8,15},{9,10},{10,... | collective-permute-start | bytes 36872 | tf_op jit(solution)/shard_map/ppermute | solution.py:483
  3.9 5.3 %collective-permute-start.1 = (f32[3,8,128]{2,1,0:T(8,128)S(1)}, f32[3,8,128]{2,1,0:T(8,128)S(1)}, u32[]{:S(2)}, u32[]{:S(2)}) collective-permute-start(f32[3,8,128]{2,1,0:T(8,128)S(1)} %get-tuple-element.19), channel_id=1, source_target_pairs={{0,1},{1,0},{2,3},{3,2},{4,5},{5,4},{6,7},{7,6},{8,9},{9,8},{10,11... | collective-permute-start | bytes 36872 | tf_op jit(solution)/shard_map/ppermute | solution.py:483
  10.4 13.0 %collective-permute-start.2 = (f32[24,9,4,128]{3,2,1,0:T(4,128)S(1)}, f32[24,9,4,128]{3,2,1,0:T(4,128)S(1)}, u32[]{:S(2)}, u32[]{:S(2)}) collective-permute-start(f32[24,9,4,128]{3,2,1,0:T(4,128)S(1)} %get-tuple-element.22), channel_id=1, source_target_pairs={{0,248},{8,16},{16,8},{24,32},{32,24},{40,48},{48,40},{56,64},{64,... | collective-permute-start | bytes 1327112 | tf_op jit(solution)/shard_map/ppermute | solution.py:483
  17.4 6.0 %collective-permute-start.3 = (f32[24,9,4,128]{3,2,1,0:T(4,128)S(1)}, f32[24,9,4,128]{3,2,1,0:T(4,128)S(1)}, u32[]{:S(2)}, u32[]{:S(2)}) collective-permute-start(f32[24,9,4,128]{3,2,1,0:T(4,128)S(1)} %get-tuple-element.23), channel_id=1, source_target_pairs={{0,8},{8,0},{16,24},{24,16},{32,40},{40,32},{48,56},{56,48},{64,72... | collective-permute-start | bytes 1327112 | tf_op jit(solution)/shard_map/ppermute | solution.py:483

commit v2 on v1

--- a/solution.py
+++ b/solution.py
@@ -56,58 +56,54 @@
     def plane(a):
         big, small = f[a] + f[a + 1], f[a] - f[a + 1]
         big2, small2 = f[a + 2] + f[a + 3], f[a + 2] - f[a + 3]
-        return big + big2, big - big2, small + small2, small - small2
-
-    nxy, mxy, tyyx, txxy = plane(7)
-    nxz, mxz, tzzx, txxz = plane(11)
-    nyz, myz, tzzy, tyyz = plane(15)
-    jx = dx + (tyyx + tzzx)
-    jy = dy + (txxy + tzzy)
-    jz = dz + (txxz + tyyz)
-    mxx = sx + (nxy + nxz)
-    myy = sy + (nxy + nyz)
-    mzz = sz + (nxz + nyz)
-    rho = ((f[0] + mxx) + (sy + sz)) + nyz
+        return big + big2, big - big2, small + small2, small - small2, (small, small2)
+
+    nxy, mxy, tyyx, txxy, odd_xy = plane(7)
+    nxz, mxz, tzzx, txxz, odd_xz = plane(11)
+    nyz, myz, tzzy, tyyz, odd_yz = plane(15)
+    tx, ty, tz = tyyx + tzzx, txxy + tzzy, txxz + tyyz
+    jx, jy, jz = dx + tx, dy + ty, dz + tz
+    nx, ny, nz = nxy + nxz, nxy + nyz, nxz + nyz
+    total_s = (sx + sy) + sz
+    total_n = nx + nyz
+    rho = (f[0] + total_s) + total_n
     inv = 0.3125 / rho
     vx, vy, vz = jx * inv, jy * inv, jz * inv
     gx, gy, gz = jx * vx, jy * vy, jz * vz
-    third = rho * (1.25 / 6.0)
-    hx = (third + (gx + gx)) - 0.125 * mxx
-    hy = (third + (gy + gy)) - 0.125 * myy
-    hz = (third + (gz + gz)) - 0.125 * mzz
+    total_g = (gx + gy) + gz
     mxy = jx * vy - 0.0625 * mxy
     mxz = jx * vz - 0.0625 * mxz
     myz = jy * vz - 0.0625 * myz
-    base = rho * (1.3 / 36.0) + (gx + gy + gz) * (1.3 / 12.0 / 0.3125)
+    base = rho * (1.3 / 36.0) + total_g * (1.3 / 3.75)
     nxy = (base - 0.52 * gz) - 0.075 * nxy
     nxz = (base - 0.52 * gy) - 0.075 * nxz
     nyz = (base - 0.52 * gx) - 0.075 * nyz
     bx = jx * (0.4 / 3.0) + fx * (1.0 / 12.0)
     by = jy * (0.4 / 3.0) + fy * (1.0 / 12.0)
     bz = jz * (0.4 / 3.0) + fz * (1.0 / 12.0)
-    tyyx, tzzx = bx - 0.15 * tyyx, bx - 0.15 * tzzx
-    txxy, tzzy = by - 0.15 * txxy, by - 0.15 * tzzy
-    txxz, tyyz = bz - 0.15 * txxz, bz - 0.15 * tyyz
+    rest = rho * (1.25 / 6.0 - 5.2 / 36.0) + total_g * (1.04 - 5.2 / 3.75)
     out = [None] * 19
 
-    def axis(a, half, j, force_a, n1, n2, t1, t2):
-        even = half - 2.0 * (n1 + n2)
-        odd = 0.5 * (j + force_a) - 2.0 * (t1 + t2)
+    def axis(a, g, s, n, d, t, force_a):
+        even = ((rest + 0.96 * g) - 0.125 * s) + 0.025 * n
+        odd = (0.8 / 3.0 * t - 0.1 / 3.0 * d) + force_a * (1.0 / 6.0)
         out[a], out[a + 1] = even + odd, even - odd
 
-    def edge(a, n, m, t1, t2):
+    def edge(a, n, m, b1, b2, p, q):
         big, big2 = n + m, n - m
-        small, small2 = t1 + t2, t1 - t2
+        small, small2 = (b1 + b2) - 0.3 * p, (b1 - b2) - 0.3 * q
         out[a], out[a + 1] = big + small, big - small
         out[a + 2], out[a + 3] = big2 + small2, big2 - small2
 
-    axis(1, hx, jx, fx, nxy, nxz, tyyx, tzzx)
-    axis(3, hy, jy, fy, nxy, nyz, txxy, tzzy)
-    axis(5, hz, jz, fz, nxz, nyz, txxz, tyyz)
-    edge(7, nxy, mxy, tyyx, txxy)
-    edge(11, nxz, mxz, tzzx, txxz)
-    edge(15, nyz, myz, tzzy, tyyz)
-    out[0] = rho - 2.0 * (hx + hy + hz) + 4.0 * (nxy + nxz + nyz)
+    axis(1, gx, sx, nx, dx, tx, fx)
+    axis(3, gy, sy, ny, dy, ty, fy)
+    axis(5, gz, sz, nz, dz, tz, fz)
+    edge(7, nxy, mxy, bx, by, *odd_xy)
+    edge(11, nxz, mxz, bx, bz, *odd_xz)
+    edge(15, nyz, myz, by, bz, *odd_yz)
+    out[0] = (rho * (1.0 - 1.25 + 15.6 / 36.0) + total_g * (15.6 / 3.75 - 6.08)) + (
+        0.25 * total_s + 0.2 * total_n
+    )
     return out
 
 
@@ -131,33 +127,16 @@
     return pltpu.roll(jnp.where(lane == 0, after, cur), 127, axis=1)
 
 
-def stream_own(load, halo, p, t, lane, row):
-    split = halo is None
+def stream_own(load, p, t, lane, split=False):
     f = []
     for k in range(19):
         cx, cy, cz = VEL[k]
-        own = load(OPP[k], None if split and isinstance(t, int) and t == 8 else t, p)
+        own = load(OPP[k], None if split and isinstance(t, int) and t == 8 else t, p, 0)
         q = p - cx
         if k == 0 or q < 0 or q > 3:
             f.append(own)
             continue
-
-        def get(s, k=k, q=q, cy=cy):
-            v = load(k, s, q)
-            if cy == 0 or halo is None:
-                return v
-            if cy == 1:
-                at, i, sub = 7, IN.index(k), q
-            else:
-                at, i, sub = 0, IN.index(FLIP[k]), 4 + q
-            rim = jnp.broadcast_to(halo[i, s, sub : sub + 1, :], (8, 128))
-            return jnp.where(row == at, rim, v)
-
-        v = along_z(get, t, cz, lane, split)
-        if cy == 1:
-            v = pltpu.roll(v, 1, axis=0)
-        elif cy == -1:
-            v = pltpu.roll(v, 7, axis=0)
+        v = along_z(lambda s, k=k, q=q, cy=cy: load(k, s, q, cy), t, cz, lane, split)
         f.append(jnp.where(v < BIG, v, own))
     return f
 
@@ -254,7 +233,7 @@
     force = force_of(force_ref)
     force_rim = rim_force(force, row)
 
-    @pl.loop(0, 8)
+    @pl.loop(0, 8, unroll=8)
     def _(t):
         at = pl.ds(pl.multiple_of(t * 128, 128), 128)
         for p in range(4):
@@ -269,7 +248,7 @@
         for i, k in enumerate(OUT):
             e3[t, i] = edges(r1.at[k, t], r1.at[FLIP[k], t], 2, 5)
 
-    @pl.loop(1, 7)
+    @pl.loop(1, 7, unroll=6)
     def _(t):
         values = rim_values(
             lambda k, s: e1[s, k], lambda k, s: e2[s, k], lambda k, s: e3[s, OUT.index(k)],
@@ -323,28 +302,25 @@
         for i, v in enumerate(values):
             put(t, i, v)
 
-    @pl.loop(1, 7)
+    @pl.loop(1, 7, unroll=6)
     def _(t):
         for i in range(NMSG):
             put(t, i, inner[t - 1, i])
 
 
-def middle_kernel(force_ref, r1, r1h, r2_hbm, r2, sem):
-    lane, row = lanes(), rows()
+def middle_kernel(force_ref, r1, r1h, r2):
+    lane = lanes()
     force = force_of(force_ref)
 
-    def copy(t):
-        return pltpu.make_async_copy(r2.at[t], r2_hbm.at[t], sem.at[t])
-
     def step(t):
-        def get(k, s, p):
-            return r1h[k, 8 * p : 8 * p + 8, :] if s is None else r1[k, s, 8 * p : 8 * p + 8, :]
+        def get(k, s, p, cy):
+            v = r1h[k, 8 * p : 8 * p + 8, :] if s is None else r1[k, s, 8 * p : 8 * p + 8, :]
+            return pltpu.roll(v, cy % 8, axis=0) if cy else v
 
         for p in range(4):
-            g = collide(stream_own(get, None, p, t, lane, row), force)
+            g = collide(stream_own(get, p, t, lane, split=True), force)
             for k in range(19):
                 r2[t, k, 8 * p : 8 * p + 8, :] = g[k]
-        copy(t).start()
 
     for t in (0, 7, 8):
         step(t)
@@ -353,37 +329,39 @@
     def _(t):
         step(t)
 
-    for t in range(9):
-        copy(t).wait()
-
 
 def last_kernel(
-    force_ref, r2_hbm, edge, far, near, mask, density, velocity, r2, r3, got, r2h, r2e, r3h, sem
+    force_ref, r2_in, edge, far, near, mask, density, velocity, r2, r3, got, got2, r2h, r2e
 ):
-    copy = pltpu.make_async_copy(r2_hbm, r2, sem)
-    copy.start()
-
-    def load2(k, s, p):
-        return r2[s, k, 8 * p : 8 * p + 8, :]
-
-    def load3(k, s, p):
-        return r3[s, k, 8 * p : 8 * p + 8, :]
+    def load2(k, s, p, cy):
+        return r2[s, k, pl.ds(10 * p + 1 - cy, 8), :]
+
+    def load3(k, s, p, cy):
+        return r3[s, k, pl.ds(10 * p + 1 - cy, 8), :]
+
+    def around(ref, t, k, v):
+        ref[t, k, pl.ds(0, 4, stride=10), :] = v[0:4]
+        ref[t, FLIP[k], pl.ds(9, 4, stride=10), :] = v[4:8]
 
     lane, row = lanes(), rows()
     force = force_of(force_ref)
     force_rim = rim_force(force, row)
     even_y = lax.rem(lax.axis_index("gy"), 2) == 0
 
-    @pl.loop(0, 9)
-    def _(t):
-        for i in range(NMSG):
-            v = jnp.concatenate([near[i, t], far[i, t]], axis=0)
-            got[i, t] = jnp.where(even_y, pltpu.roll(v, 4, axis=0), v)
-
-    copy.wait()
-
-    @pl.loop(0, 9)
-    def _(t):
+    def received(i, t):
+        v = jnp.concatenate([near[i, t], far[i, t]], axis=0)
+        return jnp.where(even_y, pltpu.roll(v, 4, axis=0), v)
+
+    @pl.loop(0, 9, unroll=9)
+    def _(t):
+        for i in range(5):
+            got[i, t] = received(i, t)
+
+    @pl.loop(0, 9, unroll=9)
+    def _(t):
+        for k in range(19):
+            for p in range(4):
+                r2[t, k, pl.ds(10 * p + 1, 8), :] = r2_in[t, k, 8 * p : 8 * p + 8, :]
         f = [None] * 19
         for i, k in enumerate(LOCAL):
             f[k] = edge[5 + i, t]
@@ -392,23 +370,27 @@
             f[k] = stream_rim(lambda s, i=i: got[i, s], own, k, t, lane, row)
         g = collide(f, force_rim)
         for k in range(19):
-            r2[t, k, pl.ds(0, 4, stride=8), :] = g[k][0:4]
-            r2[t, FLIP[k], pl.ds(7, 4, stride=8), :] = g[k][4:8]
+            r2[t, k, pl.ds(1, 4, stride=10), :] = g[k][0:4]
+            r2[t, FLIP[k], pl.ds(8, 4, stride=10), :] = g[k][4:8]
         for i, k in enumerate(OUT):
             r2e[i, t] = g[k]
         f = [None] * 19
         for i, k in enumerate(LOCAL):
-            f[FLIP[k]] = got[5 + i, t]
+            f[FLIP[k]] = received(5 + i, t)
         for i, k in enumerate(OUT):
             own = got[IN.index(OPP[k]), t]
             f[k] = stream_rim(lambda s, i=i: edge[i, s], own, k, t, lane, row)
         g = collide(f, force_rim)
         for i, k in enumerate(IN + FLAT + OUT):
             r2h[i, t] = g[k]
+            if k in IN:
+                around(r2, t, k, g[k])
+        for i in range(5):
+            got2[i, t] = received(19 + i, t)
 
     place = {k: i for i, k in enumerate(IN + FLAT + OUT)}
 
-    @pl.loop(0, 9)
+    @pl.loop(0, 9, unroll=9)
     def _(t):
         f = [None] * 19
         for k in range(19):
@@ -418,22 +400,22 @@
             elif k in FLAT:
                 f[k] = stream_rim(lambda s, k=k: r2h[place[k], s], own, k, t, lane, row)
             elif k in IN:
-                f[k] = stream_rim(lambda s, k=k: got[19 + IN.index(k), s], own, k, t, lane, row)
+                f[k] = stream_rim(lambda s, k=k: got2[IN.index(k), s], own, k, t, lane, row)
             else:
                 f[k] = stream_rim(lambda s, k=k: r2e[OUT.index(k), s], own, k, t, lane, row)
         g = collide(f, force_rim)
-        for i, k in enumerate(IN):
-            r3h[i, t] = g[k]
+        for k in IN:
+            around(r3, t, k, g[k])
         for p in range(4):
-            g = collide(stream_own(load2, r2h, p, t, lane, row), force)
+            g = collide(stream_own(load2, p, t, lane), force)
             for k in range(19):
-                r3[t, k, 8 * p : 8 * p + 8, :] = g[k]
-
-    @pl.loop(0, 8)
+                r3[t, k, pl.ds(10 * p + 1, 8), :] = g[k]
+
+    @pl.loop(0, 8, unroll=8)
     def _(t):
         at = pl.ds(pl.multiple_of(t * 128, 128), 128)
         for p in range(4):
-            f = stream_own(load3, r3h, p, t, lane, row)
+            f = stream_own(load3, p, t, lane)
             rho = f[0]
             for k in range(1, 19):
                 rho = rho + f[k]
@@ -509,15 +491,14 @@
     near = swap(near, "gy", 0)
     r2 = call(
         middle_kernel, "middle", 3.0,
-        sds(9, 19, 32, 128), [SMEM, VMEM, VMEM], HBM,
-        [buf(9, 19, 32, 128), pltpu.SemaphoreType.DMA((9,))],
+        sds(9, 19, 32, 128), [SMEM, VMEM, VMEM], VMEM, [],
     )(force, r1, r1h)
     return call(
         last_kernel, "last", 5.0,
         (sds(4, 8, 1024), sds(3, 4, 8, 1024)),
-        [SMEM, HBM, VMEM, VMEM, VMEM, VMEM], (VMEM, VMEM),
-        [buf(9, 19, 32, 128), buf(9, 19, 32, 128), buf(NMSG, 9, 8, 128), buf(19, 9, 8, 128),
-         buf(5, 9, 8, 128), buf(5, 9, 8, 128), pltpu.SemaphoreType.DMA],
+        [SMEM] + [VMEM] * 5, (VMEM, VMEM),
+        [buf(9, 19, 40, 128), buf(9, 19, 40, 128), buf(5, 9, 8, 128), buf(5, 9, 8, 128),
+         buf(19, 9, 8, 128), buf(5, 9, 8, 128)],
     )(force, r2, edge, far, near, mask)
 
 

time: 29.6 us -> 26.6 us (0.90)
  Pallas kernels: 14.4 us -> 10.4 us
  waiting for transfers between devices: 2.9 us -> 3.91 us
    pallas_call x1, Pallas kernels: 6.11 us -> 3.74 us  [local(): call(last_kernel, 'last', 5.0, (sds(4, 8, 1024), sds(3, 4, 8, 1024)), [SM...]
    ppermute x4, waiting for transfers between devices: 2.9 us -> 3.91 us  [swap(): return lax.ppermute(x, axis, pairs)]
    pallas_call x1, Pallas kernels: 3.08 us -> 2.07 us  [local(): call(middle_kernel, 'middle', 3.0, sds(9, 19, 32, 128), [SMEM, VMEM, VMEM...]
    pallas_call x1, Pallas kernels: 2.51 us -> 1.87 us  [local(): call(collide_kernel, 'collide', 3.0, (sds(19, 8, 32, 128), sds(8, 19, 8,...]
  transfers between devices with their start and end apart: 4 -> 4, of which waited for: 1 -> 1; matrix products, arithmetic and copies ran while one was open for 0% -> 0% of each run, Pallas kernels for 19% -> 15%
where the time goes in v2:
time: 26.6 us; the launch traced here: 26.5 us
  starting transfers between devices  11.5 us (43%)
  Pallas kernels  10.4 us (39%)
  waiting for transfers between devices  3.91 us (15%)
  between operations  0.71 us (3%)
    ppermute x4, starting transfers between devices, swap(): return lax.ppermute(x, axis, pairs)  11.5 us
    ppermute x4, waiting for transfers between devices, swap(): return lax.ppermute(x, axis, pairs)  3.91 us
    pallas_call x1, Pallas kernels, local(): call(last_kernel, 'last', 5.0, (sds(4, 8, 1024), sds(3, 4, 8, 1024)), [SM...  3.74 us
    pallas_call x1, Pallas kernels, local(): call(middle_kernel, 'middle', 3.0, sds(9, 19, 32, 128), [SMEM, VMEM, VMEM...  2.07 us
    pallas_call x1, Pallas kernels, local(): call(collide_kernel, 'collide', 3.0, (sds(19, 8, 32, 128), sds(8, 19, 8,...  1.87 us
    pallas_call x1, Pallas kernels, local(): call(pack_kernel, 'pack', 0.7, (sds(3, 8, 128), sds(3, 8, 128)), [HBM, HB...  1.6 us
    pallas_call x1, Pallas kernels, local(): call(rim_kernel, 'rim', 1.0, (sds(19, 32, 128), sds(NMSG, 9, 8, 128), sds...  1.12 us
  transfers between devices with their start and end apart: 4, of which 1 were waited for; matrix products, arithmetic and copies ran while one was open for 0% of the time, Pallas kernels for 15%

profile of v2, /device:TPU:8, one launch (start us, length us, event | category | flops | bytes accessed | tf_op | source)
XLA Modules:
  0.0 26.5 jit_solution(3688604663182437854)
XLA Ops:
  0.6 0.0 copy-start.1
  0.6 0.0 copy-start
  0.6 0.0 copy-start.2
  0.7 1.6 %pack.1 = (f32[3,8,128]{2,1,0:T(8,128)S(1)}, f32[3,8,128]{2,1,0:T(8,128)S(1)}) custom-call(f32[19,4,8,1024]{3,2,1,0:T(8,128)} %pop_hbm.1, s32[4,8,1024]{2,1,0:T(8,128)} %mask.3), custom_call_target="tpu_custom_call" | custom-call | flops 700000 | bytes 2100000 | tf_op jit(solution)/shard_map/pack/pallas_call | solution.py:470
  2.3 1.7 %collective-permute-start = (f32[3,8,128]{2,1,0:T(8,128)S(1)}, f32[3,8,128]{2,1,0:T(8,128)S(1)}, u32[]{:S(2)}, u32[]{:S(2)}) collective-permute-start(f32[3,8,128]{2,1,0:T(8,128)S(1)} %get-tuple-element.18), channel_id=1, source_target_pairs={{0,7},{1,2},{2,1},{3,4},{4,3},{5,6},{6,5},{7,0},{8,15},{9,10},{10,... | collective-permute-start | bytes 36872 | tf_op jit(solution)/shard_map/ppermute | solution.py:465
  3.9 2.8 %collective-permute-start.1 = (f32[3,8,128]{2,1,0:T(8,128)S(1)}, f32[3,8,128]{2,1,0:T(8,128)S(1)}, u32[]{:S(2)}, u32[]{:S(2)}) collective-permute-start(f32[3,8,128]{2,1,0:T(8,128)S(1)} %get-tuple-element.19), channel_id=1, source_target_pairs={{0,1},{1,0},{2,3},{3,2},{4,5},{5,4},{6,7},{7,6},{8,9},{9,8},{10,11... | collective-permute-start | bytes 36872 | tf_op jit(solution)/shard_map/ppermute | solution.py:465
  6.7 0.0 copy-done.1
  6.7 0.0 copy-done
  6.8 0.0 copy-done.2
  6.8 1.9 %collide.1 = (f32[19,8,32,128]{3,2,1,0:T(8,128)S(1)}, f32[8,19,8,128]{3,2,1,0:T(8,128)S(1)}, f32[8,19,8,128]{3,2,1,0:T(8,128)S(1)}, f32[8,5,8,128]{3,2,1,0:T(8,128)S(1)}, f32[6,24,8,128]{3,2,1,0:T(8,128)S(1)}) custom-call(f32[3]{0:T(128)S(1)} %copy-done.2, f32[19,4,8,1024]{3,2,1,0:T(8,128)S(1)} %copy-done, s32[4,8,1024]{2,1,0:T(8,128)S(1)} %copy-done.1), custom_call_target="tpu_custom_call" | custom-call | flops 3000000 | bytes 9000000 | tf_op jit(solution)/shard_map/collide/pallas_call | solution.py:478
  8.6 0.0 collective-permute-done.got1
  8.6 0.0 collective-permute-done.1.got0
  8.6 1.1 %rim.1 = (f32[19,32,128]{2,1,0:T(8,128)S(1)}, f32[24,9,8,128]{3,2,1,0:T(8,128)S(1)}, f32[24,9,4,128]{3,2,1,0:T(4,128)S(1)}, f32[24,9,4,128]{3,2,1,0:T(4,128)S(1)}) custom-call(f32[3]{0:T(128)S(1)} %copy-done.2, f32[8,19,8,128]{3,2,1,0:T(8,128)S(1)} %get-tuple-element.14.e1, f32[8,19,8,128]{3,2,1,0:T(8,128)S(1)} %get-tuple-element.15.e2, ...), custom_call_target="tpu_custom_call" | custom-call | flops 1000000 | bytes 3000000 | tf_op jit(solution)/shard_map/rim/pallas_call | solution.py:484
  9.8 7.0 %collective-permute-start.2 = (f32[24,9,4,128]{3,2,1,0:T(4,128)S(1)}, f32[24,9,4,128]{3,2,1,0:T(4,128)S(1)}, u32[]{:S(2)}, u32[]{:S(2)}) collective-permute-start(f32[24,9,4,128]{3,2,1,0:T(4,128)S(1)} %get-tuple-element.22), channel_id=1, source_target_pairs={{0,248},{8,16},{16,8},{24,32},{32,24},{40,48},{48,40},{56,64},{64,... | collective-permute-start | bytes 1327112 | tf_op jit(solution)/shard_map/ppermute | solution.py:465
  16.8 0.0 collective-permute-start.3
  16.8 2.1 %middle.1.r2_in = f32[9,19,32,128]{3,2,1,0:T(8,128)S(1)} custom-call(f32[3]{0:T(128)S(1)} %copy-done.2, f32[19,8,32,128]{3,2,1,0:T(8,128)S(1)} %get-tuple-element.13.r1, f32[19,32,128]{2,1,0:T(8,128)S(1)} %get-tuple-element.20.r1h), custom_call_target="tpu_custom_call" | custom-call | flops 3000000 | bytes 9000000 | tf_op jit(solution)/shard_map/middle/pallas_call | solution.py:492
  18.8 3.9 %collective-permute-done.2.far = f32[24,9,4,128]{3,2,1,0:T(4,128)S(1)} collective-permute-done((f32[24,9,4,128]{3,2,1,0:T(4,128)S(1)}, f32[24,9,4,128]{3,2,1,0:T(4,128)S(1)}, u32[]{:S(2)}, u32[]{:S(2)}) %collective-permute-start.2) | collective-permute-done | bytes 442400 | tf_op jit(solution)/shard_map/ppermute | solution.py:465
  22.8 0.0 collective-permute-done.3.near
  22.8 3.7 %last.1 = (f32[4,8,1024]{2,1,0:T(8,128)}, f32[3,4,8,1024]{3,2,1,0:T(8,128)}) custom-call(f32[3]{0:T(128)S(1)} %copy-done.2, f32[9,19,32,128]{3,2,1,0:T(8,128)S(1)} %middle.1.r2_in, f32[24,9,8,128]{3,2,1,0:T(8,128)S(1)} %get-tuple-element.21.edge, f32[24,9,4,128]{3,2,1,0:T(4,128)S(1)} %collective-permute-done.2.far, ...), custom_call_target="tpu_custom_call" | custom-call | flops 5000000 | bytes 15000000 | tf_op jit(solution)/shard_map/last/pallas_call | solution.py:496
Async XLA Ops:
  0.6 6.1 %copy-start.1 = (s32[4,8,1024]{2,1,0:T(8,128)S(1)}, s32[4,8,1024]{2,1,0:T(8,128)}, u32[]{:S(2)}) copy-start(s32[4,8,1024]{2,1,0:T(8,128)} %mask.3) | copy-start | bytes 393220
  0.6 6.1 %copy-start = (f32[19,4,8,1024]{3,2,1,0:T(8,128)S(1)}, f32[19,4,8,1024]{3,2,1,0:T(8,128)}, u32[]{:S(2)}) copy-start(f32[19,4,8,1024]{3,2,1,0:T(8,128)} %pop_hbm.1) | copy-start | bytes 7471108
  0.6 6.1 %copy-start.2 = (f32[3]{0:T(128)S(1)}, f32[3]{0:T(128)}, u32[]{:S(2)}) copy-start(f32[3]{0:T(128)} %force_ref.7) | copy-start | bytes 40
  2.3 6.4 %collective-permute-start = (f32[3,8,128]{2,1,0:T(8,128)S(1)}, f32[3,8,128]{2,1,0:T(8,128)S(1)}, u32[]{:S(2)}, u32[]{:S(2)}) collective-permute-start(f32[3,8,128]{2,1,0:T(8,128)S(1)} %get-tuple-element.18), channel_id=1, source_target_pairs={{0,7},{1,2},{2,1},{3,4},{4,3},{5,6},{6,5},{7,0},{8,15},{9,10},{10,... | collective-permute-start | bytes 36872 | tf_op jit(solution)/shard_map/ppermute | solution.py:465
  3.9 4.7 %collective-permute-start.1 = (f32[3,8,128]{2,1,0:T(8,128)S(1)}, f32[3,8,128]{2,1,0:T(8,128)S(1)}, u32[]{:S(2)}, u32[]{:S(2)}) collective-permute-start(f32[3,8,128]{2,1,0:T(8,128)S(1)} %get-tuple-element.19), channel_id=1, source_target_pairs={{0,1},{1,0},{2,3},{3,2},{4,5},{5,4},{6,7},{7,6},{8,9},{9,8},{10,11... | collective-permute-start | bytes 36872 | tf_op jit(solution)/shard_map/ppermute | solution.py:465
  9.8 13.0 %collective-permute-start.2 = (f32[24,9,4,128]{3,2,1,0:T(4,128)S(1)}, f32[24,9,4,128]{3,2,1,0:T(4,128)S(1)}, u32[]{:S(2)}, u32[]{:S(2)}) collective-permute-start(f32[24,9,4,128]{3,2,1,0:T(4,128)S(1)} %get-tuple-element.22), channel_id=1, source_target_pairs={{0,248},{8,16},{16,8},{24,32},{32,24},{40,48},{48,40},{56,64},{64,... | collective-permute-start | bytes 1327112 | tf_op jit(solution)/shard_map/ppermute | solution.py:465
  16.8 6.0 %collective-permute-start.3 = (f32[24,9,4,128]{3,2,1,0:T(4,128)S(1)}, f32[24,9,4,128]{3,2,1,0:T(4,128)S(1)}, u32[]{:S(2)}, u32[]{:S(2)}) collective-permute-start(f32[24,9,4,128]{3,2,1,0:T(4,128)S(1)} %get-tuple-element.23), channel_id=1, source_target_pairs={{0,8},{8,0},{16,24},{24,16},{32,40},{40,32},{48,56},{56,48},{64,72... | collective-permute-start | bytes 1327112 | tf_op jit(solution)/shard_map/ppermute | solution.py:465

commit v3 on v2

--- a/solution.py
+++ b/solution.py
@@ -107,36 +107,27 @@
     return out
 
 
-def along_z(get, t, cz, lane, split=False):
-    def at(s):
-        return get(None if split and s == 8 else s)
-
-    if isinstance(t, int):
-        prev, succ = (t + 8) % 9, (t + 1) % 9
-    elif split:
-        prev, succ = t - 1, t + 1
-    else:
-        prev, succ = jnp.where(t == 0, 8, t - 1), jnp.where(t == 8, 0, t + 1)
-    cur = at(t) if isinstance(t, int) else get(t)
+def along_z(get, t, cz, lane):
+    cur = get(t)
     if cz == 0:
         return cur
     if cz == 1:
-        before = at(prev) if isinstance(t, int) else get(prev)
+        before = get((t + 8) % 9 if isinstance(t, int) else jnp.where(t == 0, 8, t - 1))
         return pltpu.roll(jnp.where(lane == 127, before, cur), 1, axis=1)
-    after = at(succ) if isinstance(t, int) else get(succ)
+    after = get((t + 1) % 9 if isinstance(t, int) else jnp.where(t == 8, 0, t + 1))
     return pltpu.roll(jnp.where(lane == 0, after, cur), 127, axis=1)
 
 
-def stream_own(load, p, t, lane, split=False):
+def stream_own(load, p, t, lane):
     f = []
     for k in range(19):
         cx, cy, cz = VEL[k]
-        own = load(OPP[k], None if split and isinstance(t, int) and t == 8 else t, p, 0)
+        own = load(OPP[k], t, p, 0)
         q = p - cx
         if k == 0 or q < 0 or q > 3:
             f.append(own)
             continue
-        v = along_z(lambda s, k=k, q=q, cy=cy: load(k, s, q, cy), t, cz, lane, split)
+        v = along_z(lambda s, k=k, q=q, cy=cy: load(k, s, q, cy), t, cz, lane)
         f.append(jnp.where(v < BIG, v, own))
     return f
 
@@ -166,13 +157,13 @@
     return fx, jnp.where(row < 4, fy, -fy), fz
 
 
-GROUPS = ((0, 5), (5, 10), (10, 15), (15, 19))
-
-
-def pack_kernel(pop_hbm, mask_hbm, out1, out0, first, last, mask_first, mask_last, sem):
+GROUPS = ((0, 10), (10, 19))
+
+
+def pack_kernel(pop_hbm, mask_hbm, force_hbm, out1, out0, mask, force, first, last, given, sem):
     copies = [
-        pltpu.make_async_copy(mask_hbm.at[:, :, 0:128], mask_first, sem.at[0]),
-        pltpu.make_async_copy(mask_hbm.at[:, :, 896:1024], mask_last, sem.at[1]),
+        pltpu.make_async_copy(mask_hbm, mask, sem.at[0]),
+        pltpu.make_async_copy(force_hbm, given, sem.at[1]),
     ]
     for i, (a, b) in enumerate(GROUPS):
         for j, (at, to) in enumerate(((0, first), (896, last))):
@@ -183,31 +174,33 @@
             )
     for copy in copies:
         copy.start()
-    for copy in copies:
-        copy.wait()
+    copies[0].wait()
+    copies[1].wait()
+    for i in range(3):
+        force[i] = jnp.full((8, 128), given[i], F32)
     lane = lanes()
     even = lax.rem(lax.axis_index("gz"), 2) == 0
-    group = lane // 4
-    for tile in range(3):
-        left = jnp.zeros((8, 128), F32)
-        right = jnp.zeros((8, 128), F32)
-        for s in range(32):
-            i = tile * 32 + s
-            if i >= 76:
-                break
-            k, p = i // 4, i % 4
-            a, b = first[k, p], last[k, p]
-            if k == 0:
-                a = jnp.where(mask_first[p] > 0, NAN, a)
-                b = jnp.where(mask_last[p] > 0, NAN, b)
-            if s:
-                a = pltpu.roll(a, 4 * s, axis=1)
-            if s != 31:
-                b = pltpu.roll(b, 4 * s + 4, axis=1)
-            left = jnp.where(group == s, a, left)
-            right = jnp.where(group == s, b, right)
-        out0[tile] = jnp.where(even, right, left)
-        out1[tile] = jnp.where(even, left, right)
+    group = lane // 8
+    left = [jnp.zeros((8, 128), F32)] * 5
+    right = [jnp.zeros((8, 128), F32)] * 5
+    for n, (k0, k1) in enumerate(GROUPS):
+        copies[2 + 2 * n].wait()
+        copies[3 + 2 * n].wait()
+        for k in range(k0, k1):
+            for p in range(4):
+                tile, s = divmod(4 * k + p, 16)
+                a, b = first[k, p], last[k, p]
+                if k == 0:
+                    a = jnp.where(mask[p, :, 0:128] > 0, NAN, a)
+                    b = jnp.where(mask[p, :, 896:1024] > 0, NAN, b)
+                if s:
+                    a = pltpu.roll(a, 8 * s, axis=1)
+                    b = pltpu.roll(b, 8 * s, axis=1)
+                left[tile] = jnp.where(group == s, a, left[tile])
+                right[tile] = jnp.where(group == (s + 15) % 16, b, right[tile])
+    for tile in range(5):
+        out0[tile] = jnp.where(even, right[tile], left[tile])
+        out1[tile] = jnp.where(even, left[tile], right[tile])
 
 
 def rim_values(e1, e2, e3, t, force_rim, lane, row):
@@ -228,28 +221,25 @@
     return values + [g[k] for k in OUT]
 
 
-def collide_kernel(force_ref, pop, mask, r1, e1, e2, e3, inner):
+def edge_kernel(force_ref, pop, mask, e1, e2, e3, inner):
     lane, row = lanes(), rows()
-    force = force_of(force_ref)
-    force_rim = rim_force(force, row)
-
-    @pl.loop(0, 8, unroll=8)
-    def _(t):
-        at = pl.ds(pl.multiple_of(t * 128, 128), 128)
-        for p in range(4):
-            f = [pop[k, p, :, at] for k in range(19)]
-            f[0] = jnp.where(mask[p, :, at] > 0, NAN, f[0])
-            g = collide(f, force)
-            for k in range(19):
-                r1[k, t, 8 * p : 8 * p + 8, :] = g[k]
-        for k in range(19):
-            e1[t, k] = edges(r1.at[k, t], r1.at[FLIP[k], t], 0, 7)
-            e2[t, k] = edges(r1.at[k, t], r1.at[FLIP[k], t], 1, 6)
-        for i, k in enumerate(OUT):
-            e3[t, i] = edges(r1.at[k, t], r1.at[FLIP[k], t], 2, 5)
-
-    @pl.loop(1, 7, unroll=6)
-    def _(t):
+    force_rim = rim_force(force_of(force_ref), row)
+
+    def take(k, t, lower, upper):
+        a = pop[k, pl.ds(8 * t + lower, 4, stride=64), :]
+        b = pop[FLIP[k], pl.ds(8 * t + upper, 4, stride=64), :]
+        return jnp.concatenate([a, b], axis=0)
+
+    for t in range(8):
+        for depth, e in enumerate((e1, e2, e3)):
+            f = [take(k, t, depth, 7 - depth) for k in range(19)]
+            a = mask[pl.ds(8 * t + depth, 4, stride=64), :]
+            b = mask[pl.ds(8 * t + 7 - depth, 4, stride=64), :]
+            f[0] = jnp.where(jnp.concatenate([a, b], axis=0) > 0, NAN, f[0])
+            g = collide(f, force_rim)
+            for i, k in enumerate(OUT if depth == 2 else range(19)):
+                e[t, i] = g[k]
+    for t in range(1, 7):
         values = rim_values(
             lambda k, s: e1[s, k], lambda k, s: e2[s, k], lambda k, s: e3[s, OUT.index(k)],
             t, force_rim, lane, row,
@@ -258,41 +248,33 @@
             inner[t - 1, i] = v
 
 
-def rim_kernel(force_ref, e1, e2, e3, inner, got1, got0, r1h, edge, far, near, strip, h1, h2, h3):
+def rim_kernel(force_ref, e1, e2, e3, inner, got1, got0, strip, outer, far, near, h1, h2, h3):
     lane, row = lanes(), rows()
-    force = force_of(force_ref)
-    force_rim = rim_force(force, row)
+    force_rim = rim_force(force_of(force_ref), row)
     even_z = lax.rem(lax.axis_index("gz"), 2) == 0
     even_y = lax.rem(lax.axis_index("gy"), 2) == 0
-    for tile in range(3):
+    for tile in range(5):
         a, b = got0[tile], got1[tile]
-        from_right = jnp.where(even_z, a, b)
-        from_left = jnp.where(even_z, b, a)
-        for s in range(32):
-            i = tile * 32 + s
+        take_a = even_z == ((lane & 7) < 4)
+        both = jnp.where(take_a, a, b)
+        for s in range(16):
+            i = tile * 16 + s
             if i >= 76:
                 break
             k, p = i // 4, i % 4
-            x = pltpu.roll(from_right, 128 - 4 * s, axis=1) if s else from_right
-            y = pltpu.roll(from_left, 124 - 4 * s, axis=1) if s != 31 else from_left
-            strip[k, p] = jnp.where(lane < 64, x, y)
-    for p in range(4):
-        g = collide([strip[k, p] for k in range(19)], force)
-        for k in range(19):
-            r1h[k, 8 * p : 8 * p + 8, :] = g[k]
-    for k in range(19):
-        h1[k] = edges(r1h.at[k], r1h.at[FLIP[k]], 0, 7)
-        h2[k] = edges(r1h.at[k], r1h.at[FLIP[k]], 1, 6)
-    for i, k in enumerate(OUT):
-        h3[i] = edges(r1h.at[k], r1h.at[FLIP[k]], 2, 5)
-
-    def put(t, i, v):
-        edge[i, t] = v
+            strip[k, 8 * p : 8 * p + 8, :] = pltpu.roll(both, 128 - 8 * s, axis=1) if s else both
+    for depth, h in enumerate((h1, h2, h3)):
+        f = [edges(strip.at[k], strip.at[FLIP[k]], depth, 7 - depth) for k in range(19)]
+        g = collide(f, force_rim)
+        for i, k in enumerate(OUT if depth == 2 else range(19)):
+            h[i] = g[k]
+
+    def halves(v):
         w = jnp.where(even_y, pltpu.roll(v, 4, axis=0), v)
-        near[i, t] = w[0:4]
-        far[i, t] = w[4:8]
-
-    for t in (0, 7, 8):
+        return w[4:8], w[0:4]
+
+    packed = [jnp.zeros((8, 128), F32)] * 2
+    for t in (8, 0, 7):
         values = rim_values(
             lambda k, s: h1[k] if s == 8 else e1[s, k],
             lambda k, s: h2[k] if s == 8 else e2[s, k],
@@ -300,38 +282,53 @@
             t, force_rim, lane, row,
         )
         for i, v in enumerate(values):
-            put(t, i, v)
-
-    @pl.loop(1, 7, unroll=6)
-    def _(t):
+            if i < 19:
+                outer[(0, 7, 8).index(t), i] = v
+            if t == 8:
+                tile, s = divmod(i, 16)
+                packed[tile] = jnp.where(lane // 8 == s, pltpu.roll(v, (8 * s + 4) % 128, axis=1), packed[tile])
+            else:
+                far[8 * i + t], near[8 * i + t] = halves(v)
+    for tile in range(2):
+        far[192 + tile], near[192 + tile] = halves(packed[tile])
+    for t in range(1, 7):
         for i in range(NMSG):
-            put(t, i, inner[t - 1, i])
-
-
-def middle_kernel(force_ref, r1, r1h, r2):
+            far[8 * i + t], near[8 * i + t] = halves(inner[t - 1, i])
+
+
+def middle_kernel(force_ref, pop, mask, strip, r2, r1):
     lane = lanes()
     force = force_of(force_ref)
 
-    def step(t):
-        def get(k, s, p, cy):
-            v = r1h[k, 8 * p : 8 * p + 8, :] if s is None else r1[k, s, 8 * p : 8 * p + 8, :]
-            return pltpu.roll(v, cy % 8, axis=0) if cy else v
-
+    @pl.loop(0, 8, unroll=2)
+    def _(t):
         for p in range(4):
-            g = collide(stream_own(get, p, t, lane, split=True), force)
+            at = pl.ds(pl.multiple_of(64 * p + 8 * t, 8), 8)
+            f = [pop[k, at, :] for k in range(19)]
+            f[0] = jnp.where(mask[at, :] > 0, NAN, f[0])
+            g = collide(f, force)
+            for k in range(19):
+                r1[t, k, 8 * p : 8 * p + 8, :] = g[k]
+
+    for p in range(4):
+        g = collide([strip[k, 8 * p : 8 * p + 8, :] for k in range(19)], force)
+        for k in range(19):
+            r1[8, k, 8 * p : 8 * p + 8, :] = g[k]
+
+    def load(k, s, p, cy):
+        v = r1[s, k, 8 * p : 8 * p + 8, :]
+        return pltpu.roll(v, cy % 8, axis=0) if cy else v
+
+    @pl.loop(0, 9, unroll=3)
+    def _(t):
+        for p in range(4):
+            g = collide(stream_own(load, p, t, lane), force)
             for k in range(19):
                 r2[t, k, 8 * p : 8 * p + 8, :] = g[k]
 
-    for t in (0, 7, 8):
-        step(t)
-
-    @pl.loop(1, 7)
-    def _(t):
-        step(t)
-
 
 def last_kernel(
-    force_ref, r2_in, edge, far, near, mask, density, velocity, r2, r3, got, got2, r2h, r2e
+    force_ref, r2_in, inner, outer, far, near, mask, density, velocity, r2, r3, got, got2, r2h, r2e
 ):
     def load2(k, s, p, cy):
         return r2[s, k, pl.ds(10 * p + 1 - cy, 8), :]
@@ -348,25 +345,34 @@
     force_rim = rim_force(force, row)
     even_y = lax.rem(lax.axis_index("gy"), 2) == 0
 
+    def halves(at):
+        v = jnp.concatenate([near[at], far[at]], axis=0)
+        return jnp.where(even_y, pltpu.roll(v, 4, axis=0), v)
+
+    packed = [halves(192), halves(193)]
+
     def received(i, t):
-        v = jnp.concatenate([near[i, t], far[i, t]], axis=0)
-        return jnp.where(even_y, pltpu.roll(v, 4, axis=0), v)
-
-    @pl.loop(0, 9, unroll=9)
-    def _(t):
+        if t < 8:
+            return halves(8 * i + t)
+        tile, s = divmod(i, 16)
+        return pltpu.roll(packed[tile], (124 - 8 * s) % 128, axis=1)
+
+    def edge(i, t):
+        return outer[(0, 7, 8).index(t), i] if t in (0, 7, 8) else inner[t - 1, i]
+
+    for t in range(9):
         for i in range(5):
             got[i, t] = received(i, t)
 
-    @pl.loop(0, 9, unroll=9)
-    def _(t):
+    for t in range(9):
         for k in range(19):
             for p in range(4):
                 r2[t, k, pl.ds(10 * p + 1, 8), :] = r2_in[t, k, 8 * p : 8 * p + 8, :]
         f = [None] * 19
         for i, k in enumerate(LOCAL):
-            f[k] = edge[5 + i, t]
+            f[k] = edge(5 + i, t)
         for i, k in enumerate(IN):
-            own = edge[OUT.index(OPP[k]), t]
+            own = edge(OUT.index(OPP[k]), t)
             f[k] = stream_rim(lambda s, i=i: got[i, s], own, k, t, lane, row)
         g = collide(f, force_rim)
         for k in range(19):
@@ -379,7 +385,7 @@
             f[FLIP[k]] = received(5 + i, t)
         for i, k in enumerate(OUT):
             own = got[IN.index(OPP[k]), t]
-            f[k] = stream_rim(lambda s, i=i: edge[i, s], own, k, t, lane, row)
+            f[k] = stream_rim(lambda s, i=i: edge(i, s), own, k, t, lane, row)
         g = collide(f, force_rim)
         for i, k in enumerate(IN + FLAT + OUT):
             r2h[i, t] = g[k]
@@ -390,8 +396,7 @@
 
     place = {k: i for i, k in enumerate(IN + FLAT + OUT)}
 
-    @pl.loop(0, 9, unroll=9)
-    def _(t):
+    for t in range(9):
         f = [None] * 19
         for k in range(19):
             own = r2h[place[OPP[k]], t]
@@ -411,9 +416,8 @@
             for k in range(19):
                 r3[t, k, pl.ds(10 * p + 1, 8), :] = g[k]
 
-    @pl.loop(0, 8, unroll=8)
-    def _(t):
-        at = pl.ds(pl.multiple_of(t * 128, 128), 128)
+    for t in range(8):
+        at = pl.ds(t * 128, 128)
         for p in range(4):
             f = stream_own(load3, p, t, lane)
             rho = f[0]
@@ -432,7 +436,6 @@
 
 
 VMEM = pl.BlockSpec(memory_space=pltpu.VMEM)
-SMEM = pl.BlockSpec(memory_space=pltpu.SMEM)
 HBM = pl.BlockSpec(memory_space=pltpu.HBM)
 
 
@@ -465,41 +468,50 @@
     return lax.ppermute(x, axis, pairs)
 
 
+def tiles(x):
+    lead = x.shape[:-3]
+    planes, height, width = x.shape[-3:]
+    x = x.reshape(lead + (planes, height, width // 128, 128))
+    x = jnp.swapaxes(x, -3, -2)
+    return x.reshape(lead + (planes * height * width // 128, 128))
+
+
 def local(pop, mask, force):
-    far_memory = [pltpu.with_memory_space_constraint(x, pltpu.HBM) for x in (pop, mask)]
-    z1, z0 = call(
+    far_memory = [pltpu.with_memory_space_constraint(x, pltpu.HBM) for x in (pop, mask, force)]
+    z1, z0, mask, force = call(
         pack_kernel, "pack", 0.7,
-        (sds(3, 8, 128), sds(3, 8, 128)), [HBM, HBM], (VMEM, VMEM),
-        [buf(19, 4, 8, 128), buf(19, 4, 8, 128), pltpu.VMEM((4, 8, 128), jnp.int32),
-         pltpu.VMEM((4, 8, 128), jnp.int32), pltpu.SemaphoreType.DMA((10,))],
+        (sds(5, 8, 128), sds(5, 8, 128), jax.ShapeDtypeStruct(mask.shape, mask.dtype), sds(3, 8, 128)),
+        [HBM] * 3, (VMEM,) * 4,
+        [buf(19, 4, 8, 128), buf(19, 4, 8, 128), pltpu.SMEM((3,), F32),
+         pltpu.SemaphoreType.DMA((2 + 2 * len(GROUPS),))],
     )(*far_memory)
     got1 = swap(z1, "gz", 1)
     got0 = swap(z0, "gz", 0)
-    r1, e1, e2, e3, inner = call(
-        collide_kernel, "collide", 3.0,
-        (sds(19, 8, 32, 128), sds(8, 19, 8, 128), sds(8, 19, 8, 128), sds(8, 5, 8, 128),
-         sds(6, NMSG, 8, 128)),
-        [SMEM, VMEM, VMEM], (VMEM,) * 5, [],
-    )(force, pop, mask)
-    r1h, edge, far, near = call(
+    pop_tiles, mask_tiles = tiles(pop), tiles(mask)
+    e1, e2, e3, inner = call(
+        edge_kernel, "edge", 2.0,
+        (sds(8, 19, 8, 128), sds(8, 19, 8, 128), sds(8, 5, 8, 128), sds(6, NMSG, 8, 128)),
+        [VMEM] * 3, (VMEM,) * 4, [],
+    )(force, pop_tiles, mask_tiles)
+    strip, outer, far, near = call(
         rim_kernel, "rim", 1.0,
-        (sds(19, 32, 128), sds(NMSG, 9, 8, 128), sds(NMSG, 9, 4, 128), sds(NMSG, 9, 4, 128)),
-        [SMEM] + [VMEM] * 6, (VMEM,) * 4,
-        [buf(19, 4, 8, 128), buf(19, 8, 128), buf(19, 8, 128), buf(5, 8, 128)],
+        (sds(19, 32, 128), sds(3, 19, 8, 128), sds(194, 4, 128), sds(194, 4, 128)),
+        [VMEM] * 7, (VMEM,) * 4,
+        [buf(19, 8, 128), buf(19, 8, 128), buf(5, 8, 128)],
     )(force, e1, e2, e3, inner, got1, got0)
     far = swap(far, "gy", 1)
     near = swap(near, "gy", 0)
     r2 = call(
         middle_kernel, "middle", 3.0,
-        sds(9, 19, 32, 128), [SMEM, VMEM, VMEM], VMEM, [],
-    )(force, r1, r1h)
+        sds(9, 19, 32, 128), [VMEM] * 4, VMEM, [buf(9, 19, 32, 128)],
+    )(force, pop_tiles, mask_tiles, strip)
     return call(
-        last_kernel, "last", 5.0,
+        last_kernel, "last", 4.0,
         (sds(4, 8, 1024), sds(3, 4, 8, 1024)),
-        [SMEM] + [VMEM] * 5, (VMEM, VMEM),
+        [VMEM] * 7, (VMEM, VMEM),
         [buf(9, 19, 40, 128), buf(9, 19, 40, 128), buf(5, 9, 8, 128), buf(5, 9, 8, 128),
          buf(19, 9, 8, 128), buf(5, 9, 8, 128)],
-    )(force, r2, edge, far, near, mask)
+    )(force, r2, inner, outer, far, near, mask)
 
 
 def solution(mesh):

time: 26.6 us -> 24.9 us (0.936)
  Pallas kernels: 10.4 us -> 9.5 us
  waiting for transfers between devices: 3.91 us -> 3.17 us
    pallas_call x5, Pallas kernels: 10.4 us -> 9.5 us  [the longest x1 3.27 us: local(): call(last_kernel, 'last', 4.0, (sds(4, 8, 1024), sds(3, 4, 8, 1024)), [VM...]
    ppermute x4, waiting for transfers between devices: 3.91 us -> 3.17 us  [swap(): return lax.ppermute(x, axis, pairs)]
  transfers between devices with their start and end apart: 4 -> 4, of which waited for: 1 -> 1; matrix products, arithmetic and copies ran while one was open for 0% -> 0% of each run, Pallas kernels for 15% -> 17%
where the time goes in v3:
time: 24.9 us; the launch traced here: 24.8 us
  starting transfers between devices  11.5 us (46%)
  Pallas kernels  9.5 us (38%)
  waiting for transfers between devices  3.17 us (13%)
  between operations  0.69 us (3%)
    ppermute x4, starting transfers between devices, swap(): return lax.ppermute(x, axis, pairs)  11.5 us
    pallas_call x1, Pallas kernels, local(): call(last_kernel, 'last', 4.0, (sds(4, 8, 1024), sds(3, 4, 8, 1024)), [VM...  3.27 us
    ppermute x4, waiting for transfers between devices, swap(): return lax.ppermute(x, axis, pairs)  3.17 us
    pallas_call x1, Pallas kernels, local(): call(middle_kernel, 'middle', 3.0, sds(9, 19, 32, 128), [VMEM] * 4, VMEM,...  2.33 us
    pallas_call x1, Pallas kernels, local(): call(edge_kernel, 'edge', 2.0, (sds(8, 19, 8, 128), sds(8, 19, 8, 128), s...  1.9 us
    pallas_call x1, Pallas kernels, local(): call(pack_kernel, 'pack', 0.7, (sds(5, 8, 128), sds(5, 8, 128), jax.Shape...  1.55 us
  transfers between devices with their start and end apart: 4, of which 1 were waited for; matrix products, arithmetic and copies ran while one was open for 0% of the time, Pallas kernels for 17%

profile of v3, /device:TPU:8, one launch (start us, length us, event | category | flops | bytes accessed | tf_op | source)
XLA Modules:
  0.0 24.8 jit_solution(11580748796910501369)
XLA Ops:
  0.6 0.0 copy-start
  0.6 1.6 %pack.1 = (f32[5,8,128]{2,1,0:T(8,128)S(1)}, f32[5,8,128]{2,1,0:T(8,128)S(1)}, s32[4,8,1024]{2,1,0:T(8,128)S(1)}, f32[3,8,128]{2,1,0:T(8,128)S(1)}) custom-call(f32[19,4,8,1024]{3,2,1,0:T(8,128)} %pop_hbm.1, s32[4,8,1024]{2,1,0:T(8,128)} %mask_hbm.1, f32[3]{0:T(128)} %force_hbm.1), custom_call_target="tpu_custom_call" | custom-call | flops 700000 | bytes 2100000 | tf_op jit(solution)/shard_map/pack/pallas_call | solution.py:481
  2.2 1.7 %collective-permute-start = (f32[5,8,128]{2,1,0:T(8,128)S(1)}, f32[5,8,128]{2,1,0:T(8,128)S(1)}, u32[]{:S(2)}, u32[]{:S(2)}) collective-permute-start(f32[5,8,128]{2,1,0:T(8,128)S(1)} %get-tuple-element.20), channel_id=1, source_target_pairs={{0,7},{1,2},{2,1},{3,4},{4,3},{5,6},{6,5},{7,0},{8,15},{9,10},{10,... | collective-permute-start | bytes 61448 | tf_op jit(solution)/shard_map/ppermute | solution.py:468
  3.9 2.8 %collective-permute-start.1 = (f32[5,8,128]{2,1,0:T(8,128)S(1)}, f32[5,8,128]{2,1,0:T(8,128)S(1)}, u32[]{:S(2)}, u32[]{:S(2)}) collective-permute-start(f32[5,8,128]{2,1,0:T(8,128)S(1)} %get-tuple-element.21), channel_id=1, source_target_pairs={{0,1},{1,0},{2,3},{3,2},{4,5},{5,4},{6,7},{7,6},{8,9},{9,8},{10,11... | collective-permute-start | bytes 61448 | tf_op jit(solution)/shard_map/ppermute | solution.py:468
  6.7 0.0 copy-done
  6.7 1.9 %edge.1 = (f32[8,19,8,128]{3,2,1,0:T(8,128)S(1)}, f32[8,19,8,128]{3,2,1,0:T(8,128)S(1)}, f32[8,5,8,128]{3,2,1,0:T(8,128)S(1)}, f32[6,24,8,128]{3,2,1,0:T(8,128)S(1)}) custom-call(f32[3,8,128]{2,1,0:T(8,128)S(1)} %get-tuple-element.14.force_ref, f32[19,256,128]{2,1,0:T(8,128)S(1)} %bitcast.10, s32[256,128]{1,0:T(8,128)S(1)} %bitcast.12), custom_call_target="tpu_custom_call" | custom-call | flops 2000000 | bytes 6000000 | tf_op jit(solution)/shard_map/edge/pallas_call | solution.py:491
  8.6 0.0 collective-permute-done.got1
  8.6 0.0 collective-permute-done.1.got0
  8.6 0.5 %rim.1 = (f32[19,32,128]{2,1,0:T(8,128)S(1)}, f32[3,19,8,128]{3,2,1,0:T(8,128)S(1)}, f32[194,4,128]{2,1,0:T(4,128)S(1)}, f32[194,4,128]{2,1,0:T(4,128)S(1)}) custom-call(f32[3,8,128]{2,1,0:T(8,128)S(1)} %get-tuple-element.14.force_ref, f32[8,19,8,128]{3,2,1,0:T(8,128)S(1)} %get-tuple-element.16.e1, f32[8,19,8,128]{3,2,1,0:T(8,128)S(1)} %get-tuple-element.17.e2, ...), custom_call_target="tpu_custom_call" | custom-call | flops 1000000 | bytes 3000000 | tf_op jit(solution)/shard_map/rim/pallas_call | solution.py:496
  9.1 7.0 %collective-permute-start.2 = (f32[194,4,128]{2,1,0:T(4,128)S(1)}, f32[194,4,128]{2,1,0:T(4,128)S(1)}, u32[]{:S(2)}, u32[]{:S(2)}) collective-permute-start(f32[194,4,128]{2,1,0:T(4,128)S(1)} %get-tuple-element.24), channel_id=1, source_target_pairs={{0,248},{8,16},{16,8},{24,32},{32,24},{40,48},{48,40},{56,64},{64,... | collective-permute-start | bytes 1191944 | tf_op jit(solution)/shard_map/ppermute | solution.py:468
  16.1 0.0 collective-permute-start.3
  16.1 2.3 %middle.1.r2_in = f32[9,19,32,128]{3,2,1,0:T(8,128)S(1)} custom-call(f32[3,8,128]{2,1,0:T(8,128)S(1)} %get-tuple-element.14.force_ref, f32[19,256,128]{2,1,0:T(8,128)S(1)} %bitcast.11, s32[256,128]{1,0:T(8,128)S(1)} %bitcast.13, f32[19,32,128]{2,1,0:T(8,128)S(1)} %get-tuple-element.22.strip), custom_call_target="tpu_custom_call" | custom-call | flops 3000000 | bytes 9000000 | tf_op jit(solution)/shard_map/middle/pallas_call | solution.py:504
  18.4 3.2 %collective-permute-done.2.far = f32[194,4,128]{2,1,0:T(4,128)S(1)} collective-permute-done((f32[194,4,128]{2,1,0:T(4,128)S(1)}, f32[194,4,128]{2,1,0:T(4,128)S(1)}, u32[]{:S(2)}, u32[]{:S(2)}) %collective-permute-start.2) | collective-permute-done | bytes 397344 | tf_op jit(solution)/shard_map/ppermute | solution.py:468
  21.6 0.0 collective-permute-done.3.near
  21.6 3.3 %last.1 = (f32[4,8,1024]{2,1,0:T(8,128)}, f32[3,4,8,1024]{3,2,1,0:T(8,128)}) custom-call(f32[3,8,128]{2,1,0:T(8,128)S(1)} %get-tuple-element.14.force_ref, f32[9,19,32,128]{3,2,1,0:T(8,128)S(1)} %middle.1.r2_in, f32[6,24,8,128]{3,2,1,0:T(8,128)S(1)} %get-tuple-element.19.inner, f32[3,19,8,128]{3,2,1,0:T(8,128)S(1)} %get-tuple-element.23.outer, ...), custom_call_target="tpu_custom_call" | custom-call | flops 4000000 | bytes 12000000 | tf_op jit(solution)/shard_map/last/pallas_call | solution.py:508
Async XLA Ops:
  0.6 6.1 %copy-start = (f32[19,4,8,1024]{3,2,1,0:T(8,128)S(1)}, f32[19,4,8,1024]{3,2,1,0:T(8,128)}, u32[]{:S(2)}) copy-start(f32[19,4,8,1024]{3,2,1,0:T(8,128)} %pop_hbm.1) | copy-start | bytes 7471108
  2.2 6.4 %collective-permute-start = (f32[5,8,128]{2,1,0:T(8,128)S(1)}, f32[5,8,128]{2,1,0:T(8,128)S(1)}, u32[]{:S(2)}, u32[]{:S(2)}) collective-permute-start(f32[5,8,128]{2,1,0:T(8,128)S(1)} %get-tuple-element.20), channel_id=1, source_target_pairs={{0,7},{1,2},{2,1},{3,4},{4,3},{5,6},{6,5},{7,0},{8,15},{9,10},{10,... | collective-permute-start | bytes 61448 | tf_op jit(solution)/shard_map/ppermute | solution.py:468
  3.9 4.7 %collective-permute-start.1 = (f32[5,8,128]{2,1,0:T(8,128)S(1)}, f32[5,8,128]{2,1,0:T(8,128)S(1)}, u32[]{:S(2)}, u32[]{:S(2)}) collective-permute-start(f32[5,8,128]{2,1,0:T(8,128)S(1)} %get-tuple-element.21), channel_id=1, source_target_pairs={{0,1},{1,0},{2,3},{3,2},{4,5},{5,4},{6,7},{7,6},{8,9},{9,8},{10,11... | collective-permute-start | bytes 61448 | tf_op jit(solution)/shard_map/ppermute | solution.py:468
  9.1 12.5 %collective-permute-start.2 = (f32[194,4,128]{2,1,0:T(4,128)S(1)}, f32[194,4,128]{2,1,0:T(4,128)S(1)}, u32[]{:S(2)}, u32[]{:S(2)}) collective-permute-start(f32[194,4,128]{2,1,0:T(4,128)S(1)} %get-tuple-element.24), channel_id=1, source_target_pairs={{0,248},{8,16},{16,8},{24,32},{32,24},{40,48},{48,40},{56,64},{64,... | collective-permute-start | bytes 1191944 | tf_op jit(solution)/shard_map/ppermute | solution.py:468
  16.1 5.5 %collective-permute-start.3 = (f32[194,4,128]{2,1,0:T(4,128)S(1)}, f32[194,4,128]{2,1,0:T(4,128)S(1)}, u32[]{:S(2)}, u32[]{:S(2)}) collective-permute-start(f32[194,4,128]{2,1,0:T(4,128)S(1)} %get-tuple-element.25), channel_id=1, source_target_pairs={{0,8},{8,0},{16,24},{24,16},{32,40},{40,32},{48,56},{56,48},{64,72... | collective-permute-start | bytes 1191944 | tf_op jit(solution)/shard_map/ppermute | solution.py:468

commit v4 on v3

--- a/solution.py
+++ b/solution.py
@@ -223,27 +223,24 @@
 
 def edge_kernel(force_ref, pop, mask, e1, e2, e3, inner):
     lane, row = lanes(), rows()
-    force_rim = rim_force(force_of(force_ref), row)
-
-    def take(k, t, lower, upper):
-        a = pop[k, pl.ds(8 * t + lower, 4, stride=64), :]
-        b = pop[FLIP[k], pl.ds(8 * t + upper, 4, stride=64), :]
-        return jnp.concatenate([a, b], axis=0)
-
-    for t in range(8):
-        for depth, e in enumerate((e1, e2, e3)):
-            f = [take(k, t, depth, 7 - depth) for k in range(19)]
-            a = mask[pl.ds(8 * t + depth, 4, stride=64), :]
-            b = mask[pl.ds(8 * t + 7 - depth, 4, stride=64), :]
-            f[0] = jnp.where(jnp.concatenate([a, b], axis=0) > 0, NAN, f[0])
-            g = collide(f, force_rim)
-            for i, k in enumerate(OUT if depth == 2 else range(19)):
-                e[t, i] = g[k]
+    force = force_of(force_ref)
+    force_rim = rim_force(force, row)
+    mirrored = (force[0], -force[1], force[2])
+    for depth, e in enumerate((e1, e2, e3)):
+        for side in range(2):
+            for p in range(4):
+                at = pl.ds(64 * p + (7 - depth if side else depth), 8, stride=8)
+                f = [pop[FLIP[k] if side else k, at, :] for k in range(19)]
+                f[0] = jnp.where(mask[at, :] > 0, NAN, f[0])
+                g = collide(f, mirrored if side else force)
+                for i, k in enumerate(OUT if depth == 2 else range(19)):
+                    e[i, pl.ds(4 * side + p, 8, stride=8), :] = g[k]
+
+    def tile(e):
+        return lambda k, t: e[OUT.index(k) if e is e3 else k, 8 * t : 8 * t + 8, :]
+
     for t in range(1, 7):
-        values = rim_values(
-            lambda k, s: e1[s, k], lambda k, s: e2[s, k], lambda k, s: e3[s, OUT.index(k)],
-            t, force_rim, lane, row,
-        )
+        values = rim_values(tile(e1), tile(e2), tile(e3), t, force_rim, lane, row)
         for i, v in enumerate(values):
             inner[t - 1, i] = v
 
@@ -276,9 +273,9 @@
     packed = [jnp.zeros((8, 128), F32)] * 2
     for t in (8, 0, 7):
         values = rim_values(
-            lambda k, s: h1[k] if s == 8 else e1[s, k],
-            lambda k, s: h2[k] if s == 8 else e2[s, k],
-            lambda k, s: h3[OUT.index(k)] if s == 8 else e3[s, OUT.index(k)],
+            lambda k, s: h1[k] if s == 8 else e1[k, 8 * s : 8 * s + 8, :],
+            lambda k, s: h2[k] if s == 8 else e2[k, 8 * s : 8 * s + 8, :],
+            lambda k, s: h3[OUT.index(k)] if s == 8 else e3[OUT.index(k), 8 * s : 8 * s + 8, :],
             t, force_rim, lane, row,
         )
         for i, v in enumerate(values):
@@ -490,7 +487,7 @@
     pop_tiles, mask_tiles = tiles(pop), tiles(mask)
     e1, e2, e3, inner = call(
         edge_kernel, "edge", 2.0,
-        (sds(8, 19, 8, 128), sds(8, 19, 8, 128), sds(8, 5, 8, 128), sds(6, NMSG, 8, 128)),
+        (sds(19, 64, 128), sds(19, 64, 128), sds(5, 64, 128), sds(6, NMSG, 8, 128)),
         [VMEM] * 3, (VMEM,) * 4, [],
     )(force, pop_tiles, mask_tiles)
     strip, outer, far, near = call(

time: 24.9 us -> 24.5 us (0.984); the launches traced: 24.8 us -> 24.1 us
  Pallas kernels: 9.5 us -> 8.72 us
  waiting for transfers between devices: 3.17 us -> 3.78 us
  starting transfers between devices: 11.5 us -> 10.9 us
    pallas_call x1, Pallas kernels: 1.9 us -> 1.13 us  [local(): call(edge_kernel, 'edge', 2.0, (sds(19, 64, 128), sds(19, 64, 128), sds(5...]
    ppermute x4, waiting for transfers between devices: 3.17 us -> 3.78 us  [swap(): return lax.ppermute(x, axis, pairs)]
    ppermute x4, starting transfers between devices: 11.5 us -> 10.9 us  [swap(): return lax.ppermute(x, axis, pairs)]
  transfers between devices with their start and end apart: 4 -> 4, of which waited for: 1 -> 2; matrix products, arithmetic and copies ran while one was open for 0% -> 0% of each run, Pallas kernels for 17% -> 14%
where the time goes in v4:
time: 24.5 us; the launch traced here: 24.1 us
  starting transfers between devices  10.9 us (44%)
  Pallas kernels  8.72 us (36%)
  waiting for transfers between devices  3.78 us (15%)
  between operations  0.68 us (3%)
    ppermute x4, starting transfers between devices, swap(): return lax.ppermute(x, axis, pairs)  10.9 us
    ppermute x4, waiting for transfers between devices, swap(): return lax.ppermute(x, axis, pairs)  3.78 us
    pallas_call x1, Pallas kernels, local(): call(last_kernel, 'last', 4.0, (sds(4, 8, 1024), sds(3, 4, 8, 1024)), [VM...  3.27 us
    pallas_call x1, Pallas kernels, local(): call(middle_kernel, 'middle', 3.0, sds(9, 19, 32, 128), [VMEM] * 4, VMEM,...  2.33 us
    pallas_call x1, Pallas kernels, local(): call(pack_kernel, 'pack', 0.7, (sds(5, 8, 128), sds(5, 8, 128), jax.Shape...  1.55 us
    pallas_call x1, Pallas kernels, local(): call(edge_kernel, 'edge', 2.0, (sds(19, 64, 128), sds(19, 64, 128), sds(5...  1.13 us
  transfers between devices with their start and end apart: 4, of which 2 were waited for; matrix products, arithmetic and copies ran while one was open for 0% of the time, Pallas kernels for 14%

profile of v4, /device:TPU:8, one launch (start us, length us, event | category | flops | bytes accessed | tf_op | source)
XLA Modules:
  0.0 24.1 jit_solution(15964735624896272211)
XLA Ops:
  0.6 0.0 copy-start
  0.6 1.6 %pack.1 = (f32[5,8,128]{2,1,0:T(8,128)S(1)}, f32[5,8,128]{2,1,0:T(8,128)S(1)}, s32[4,8,1024]{2,1,0:T(8,128)S(1)}, f32[3,8,128]{2,1,0:T(8,128)S(1)}) custom-call(f32[19,4,8,1024]{3,2,1,0:T(8,128)} %pop_hbm.1, s32[4,8,1024]{2,1,0:T(8,128)} %mask_hbm.1, f32[3]{0:T(128)} %force_hbm.1), custom_call_target="tpu_custom_call" | custom-call | flops 700000 | bytes 2100000 | tf_op jit(solution)/shard_map/pack/pallas_call | solution.py:478
  2.2 1.7 %collective-permute-start = (f32[5,8,128]{2,1,0:T(8,128)S(1)}, f32[5,8,128]{2,1,0:T(8,128)S(1)}, u32[]{:S(2)}, u32[]{:S(2)}) collective-permute-start(f32[5,8,128]{2,1,0:T(8,128)S(1)} %get-tuple-element.20), channel_id=1, source_target_pairs={{0,7},{1,2},{2,1},{3,4},{4,3},{5,6},{6,5},{7,0},{8,15},{9,10},{10,... | collective-permute-start | bytes 61448 | tf_op jit(solution)/shard_map/ppermute | solution.py:465
  3.9 2.8 %collective-permute-start.1 = (f32[5,8,128]{2,1,0:T(8,128)S(1)}, f32[5,8,128]{2,1,0:T(8,128)S(1)}, u32[]{:S(2)}, u32[]{:S(2)}) collective-permute-start(f32[5,8,128]{2,1,0:T(8,128)S(1)} %get-tuple-element.21), channel_id=1, source_target_pairs={{0,1},{1,0},{2,3},{3,2},{4,5},{5,4},{6,7},{7,6},{8,9},{9,8},{10,11... | collective-permute-start | bytes 61448 | tf_op jit(solution)/shard_map/ppermute | solution.py:465
  6.7 0.0 copy-done
  6.7 1.1 %edge.1 = (f32[19,64,128]{2,1,0:T(8,128)S(1)}, f32[19,64,128]{2,1,0:T(8,128)S(1)}, f32[5,64,128]{2,1,0:T(8,128)S(1)}, f32[6,24,8,128]{3,2,1,0:T(8,128)S(1)}) custom-call(f32[3,8,128]{2,1,0:T(8,128)S(1)} %get-tuple-element.14.force_ref, f32[19,256,128]{2,1,0:T(8,128)S(1)} %bitcast.10, s32[256,128]{1,0:T(8,128)S(1)} %bitcast.12), custom_call_target="tpu_custom_call" | custom-call | flops 2000000 | bytes 6000000 | tf_op jit(solution)/shard_map/edge/pallas_call | solution.py:488
  7.8 0.0 collective-permute-done.got1
  7.8 0.6 %collective-permute-done.1.got0 = f32[5,8,128]{2,1,0:T(8,128)S(1)} collective-permute-done((f32[5,8,128]{2,1,0:T(8,128)S(1)}, f32[5,8,128]{2,1,0:T(8,128)S(1)}, u32[]{:S(2)}, u32[]{:S(2)}) %collective-permute-start.1) | collective-permute-done | bytes 20512 | tf_op jit(solution)/shard_map/ppermute | solution.py:465
  8.4 0.4 %rim.1 = (f32[19,32,128]{2,1,0:T(8,128)S(1)}, f32[3,19,8,128]{3,2,1,0:T(8,128)S(1)}, f32[194,4,128]{2,1,0:T(4,128)S(1)}, f32[194,4,128]{2,1,0:T(4,128)S(1)}) custom-call(f32[3,8,128]{2,1,0:T(8,128)S(1)} %get-tuple-element.14.force_ref, f32[19,64,128]{2,1,0:T(8,128)S(1)} %get-tuple-element.16.e1, f32[19,64,128]{2,1,0:T(8,128)S(1)} %get-tuple-element.17.e2, ...), custom_call_target="tpu_custom_call" | custom-call | flops 1000000 | bytes 3000000 | tf_op jit(solution)/shard_map/rim/pallas_call | solution.py:493
  8.9 6.4 %collective-permute-start.2 = (f32[194,4,128]{2,1,0:T(4,128)S(1)}, f32[194,4,128]{2,1,0:T(4,128)S(1)}, u32[]{:S(2)}, u32[]{:S(2)}) collective-permute-start(f32[194,4,128]{2,1,0:T(4,128)S(1)} %get-tuple-element.24), channel_id=1, source_target_pairs={{0,248},{8,16},{16,8},{24,32},{32,24},{40,48},{48,40},{56,64},{64,... | collective-permute-start | bytes 1191944 | tf_op jit(solution)/shard_map/ppermute | solution.py:465
  15.3 0.0 collective-permute-start.3
  15.3 2.3 %middle.1.r2_in = f32[9,19,32,128]{3,2,1,0:T(8,128)S(1)} custom-call(f32[3,8,128]{2,1,0:T(8,128)S(1)} %get-tuple-element.14.force_ref, f32[19,256,128]{2,1,0:T(8,128)S(1)} %bitcast.11, s32[256,128]{1,0:T(8,128)S(1)} %bitcast.13, f32[19,32,128]{2,1,0:T(8,128)S(1)} %get-tuple-element.22.strip), custom_call_target="tpu_custom_call" | custom-call | flops 3000000 | bytes 9000000 | tf_op jit(solution)/shard_map/middle/pallas_call | solution.py:501
  17.6 3.2 %collective-permute-done.2.far = f32[194,4,128]{2,1,0:T(4,128)S(1)} collective-permute-done((f32[194,4,128]{2,1,0:T(4,128)S(1)}, f32[194,4,128]{2,1,0:T(4,128)S(1)}, u32[]{:S(2)}, u32[]{:S(2)}) %collective-permute-start.2) | collective-permute-done | bytes 397344 | tf_op jit(solution)/shard_map/ppermute | solution.py:465
  20.8 0.0 collective-permute-done.3.near
  20.8 3.3 %last.1 = (f32[4,8,1024]{2,1,0:T(8,128)}, f32[3,4,8,1024]{3,2,1,0:T(8,128)}) custom-call(f32[3,8,128]{2,1,0:T(8,128)S(1)} %get-tuple-element.14.force_ref, f32[9,19,32,128]{3,2,1,0:T(8,128)S(1)} %middle.1.r2_in, f32[6,24,8,128]{3,2,1,0:T(8,128)S(1)} %get-tuple-element.19.inner, f32[3,19,8,128]{3,2,1,0:T(8,128)S(1)} %get-tuple-element.23.outer, ...), custom_call_target="tpu_custom_call" | custom-call | flops 4000000 | bytes 12000000 | tf_op jit(solution)/shard_map/last/pallas_call | solution.py:505
Async XLA Ops:
  0.6 6.1 %copy-start = (f32[19,4,8,1024]{3,2,1,0:T(8,128)S(1)}, f32[19,4,8,1024]{3,2,1,0:T(8,128)}, u32[]{:S(2)}) copy-start(f32[19,4,8,1024]{3,2,1,0:T(8,128)} %pop_hbm.1) | copy-start | bytes 7471108
  2.2 5.6 %collective-permute-start = (f32[5,8,128]{2,1,0:T(8,128)S(1)}, f32[5,8,128]{2,1,0:T(8,128)S(1)}, u32[]{:S(2)}, u32[]{:S(2)}) collective-permute-start(f32[5,8,128]{2,1,0:T(8,128)S(1)} %get-tuple-element.20), channel_id=1, source_target_pairs={{0,7},{1,2},{2,1},{3,4},{4,3},{5,6},{6,5},{7,0},{8,15},{9,10},{10,... | collective-permute-start | bytes 61448 | tf_op jit(solution)/shard_map/ppermute | solution.py:465
  3.9 4.6 %collective-permute-start.1 = (f32[5,8,128]{2,1,0:T(8,128)S(1)}, f32[5,8,128]{2,1,0:T(8,128)S(1)}, u32[]{:S(2)}, u32[]{:S(2)}) collective-permute-start(f32[5,8,128]{2,1,0:T(8,128)S(1)} %get-tuple-element.21), channel_id=1, source_target_pairs={{0,1},{1,0},{2,3},{3,2},{4,5},{5,4},{6,7},{7,6},{8,9},{9,8},{10,11... | collective-permute-start | bytes 61448 | tf_op jit(solution)/shard_map/ppermute | solution.py:465
  8.9 11.9 %collective-permute-start.2 = (f32[194,4,128]{2,1,0:T(4,128)S(1)}, f32[194,4,128]{2,1,0:T(4,128)S(1)}, u32[]{:S(2)}, u32[]{:S(2)}) collective-permute-start(f32[194,4,128]{2,1,0:T(4,128)S(1)} %get-tuple-element.24), channel_id=1, source_target_pairs={{0,248},{8,16},{16,8},{24,32},{32,24},{40,48},{48,40},{56,64},{64,... | collective-permute-start | bytes 1191944 | tf_op jit(solution)/shard_map/ppermute | solution.py:465
  15.3 5.5 %collective-permute-start.3 = (f32[194,4,128]{2,1,0:T(4,128)S(1)}, f32[194,4,128]{2,1,0:T(4,128)S(1)}, u32[]{:S(2)}, u32[]{:S(2)}) collective-permute-start(f32[194,4,128]{2,1,0:T(4,128)S(1)} %get-tuple-element.25), channel_id=1, source_target_pairs={{0,8},{8,0},{16,24},{24,16},{32,40},{40,32},{48,56},{56,48},{64,72... | collective-permute-start | bytes 1191944 | tf_op jit(solution)/shard_map/ppermute | solution.py:465

commit v5 on v4

--- a/solution.py
+++ b/solution.py
@@ -221,7 +221,20 @@
     return values + [g[k] for k in OUT]
 
 
-def edge_kernel(force_ref, pop, mask, e1, e2, e3, inner):
+OWN = 4
+
+
+def relax_own(t, force, pop, mask, r1):
+    for p in range(4):
+        at = pl.ds(64 * p + 8 * t, 8)
+        f = [pop[k, at, :] for k in range(19)]
+        f[0] = jnp.where(mask[at, :] > 0, NAN, f[0])
+        g = collide(f, force)
+        for k in range(19):
+            r1[t - (OWN if t >= OWN else 0), k, 8 * p : 8 * p + 8, :] = g[k]
+
+
+def edge_kernel(force_ref, pop, mask, e1, e2, e3, inner, r1):
     lane, row = lanes(), rows()
     force = force_of(force_ref)
     force_rim = rim_force(force, row)
@@ -243,6 +256,8 @@
         values = rim_values(tile(e1), tile(e2), tile(e3), t, force_rim, lane, row)
         for i, v in enumerate(values):
             inner[t - 1, i] = v
+    for t in range(OWN):
+        relax_own(t, force, pop, mask, r1)
 
 
 def rim_kernel(force_ref, e1, e2, e3, inner, got1, got0, strip, outer, far, near, h1, h2, h3):
@@ -293,49 +308,52 @@
             far[8 * i + t], near[8 * i + t] = halves(inner[t - 1, i])
 
 
-def middle_kernel(force_ref, pop, mask, strip, r2, r1):
+def middle_kernel(force_ref, pop, mask, r1, strip, r3, second, third, rest, last_tile, r2):
     lane = lanes()
     force = force_of(force_ref)
 
-    @pl.loop(0, 8, unroll=2)
-    def _(t):
-        for p in range(4):
-            at = pl.ds(pl.multiple_of(64 * p + 8 * t, 8), 8)
-            f = [pop[k, at, :] for k in range(19)]
-            f[0] = jnp.where(mask[at, :] > 0, NAN, f[0])
-            g = collide(f, force)
-            for k in range(19):
-                r1[t, k, 8 * p : 8 * p + 8, :] = g[k]
-
+    for t in range(OWN, 8):
+        relax_own(t, force, pop, mask, rest)
     for p in range(4):
         g = collide([strip[k, 8 * p : 8 * p + 8, :] for k in range(19)], force)
         for k in range(19):
-            r1[8, k, 8 * p : 8 * p + 8, :] = g[k]
-
-    def load(k, s, p, cy):
-        v = r1[s, k, 8 * p : 8 * p + 8, :]
+            last_tile[k, 8 * p : 8 * p + 8, :] = g[k]
+
+    def load1(k, s, p, cy):
+        v = (last_tile if s == 8 else r1.at[s] if s < OWN else rest.at[s - OWN])[k, 8 * p : 8 * p + 8, :]
         return pltpu.roll(v, cy % 8, axis=0) if cy else v
 
-    @pl.loop(0, 9, unroll=3)
-    def _(t):
-        for p in range(4):
-            g = collide(stream_own(load, p, t, lane), force)
-            for k in range(19):
-                r2[t, k, 8 * p : 8 * p + 8, :] = g[k]
+    def load2(k, s, p, cy):
+        v = r2[s, k, 8 * p : 8 * p + 8, :]
+        return pltpu.roll(v, cy % 8, axis=0) if cy else v
+
+    for load, after in ((load1, r2), (load2, r3)):
+        for t in range(9):
+            for p in range(4):
+                g = collide(stream_own(load, p, t, lane), force)
+                for k in range(19):
+                    after[t, k, 8 * p : 8 * p + 8, :] = g[k]
+
+    for t in range(9):
+        for k in range(19):
+            second[k, t] = edges(r2.at[t, k], r2.at[t, FLIP[k]], 1, 6)
+        for i, k in enumerate(OUT):
+            third[i, t] = edges(r2.at[t, k], r2.at[t, FLIP[k]], 2, 5)
+
+
+WRITE = 2
 
 
 def last_kernel(
-    force_ref, r2_in, inner, outer, far, near, mask, density, velocity, r2, r3, got, got2, r2h, r2e
+    force_ref, r3_in, second, third, inner, outer, far, near, mask, density_hbm, velocity_hbm,
+    r3, got, got2, r2h, r2e, density, velocity, sem
 ):
-    def load2(k, s, p, cy):
-        return r2[s, k, pl.ds(10 * p + 1 - cy, 8), :]
-
     def load3(k, s, p, cy):
         return r3[s, k, pl.ds(10 * p + 1 - cy, 8), :]
 
-    def around(ref, t, k, v):
-        ref[t, k, pl.ds(0, 4, stride=10), :] = v[0:4]
-        ref[t, FLIP[k], pl.ds(9, 4, stride=10), :] = v[4:8]
+    def put(t, k, v, depth):
+        r3[t, k, pl.ds(depth, 4, stride=10), :] = v[0:4]
+        r3[t, FLIP[k], pl.ds(9 - depth, 4, stride=10), :] = v[4:8]
 
     lane, row = lanes(), rows()
     force = force_of(force_ref)
@@ -364,7 +382,7 @@
     for t in range(9):
         for k in range(19):
             for p in range(4):
-                r2[t, k, pl.ds(10 * p + 1, 8), :] = r2_in[t, k, 8 * p : 8 * p + 8, :]
+                r3[t, k, pl.ds(10 * p + 1, 8), :] = r3_in[t, k, 8 * p : 8 * p + 8, :]
         f = [None] * 19
         for i, k in enumerate(LOCAL):
             f[k] = edge(5 + i, t)
@@ -373,10 +391,7 @@
             f[k] = stream_rim(lambda s, i=i: got[i, s], own, k, t, lane, row)
         g = collide(f, force_rim)
         for k in range(19):
-            r2[t, k, pl.ds(1, 4, stride=10), :] = g[k][0:4]
-            r2[t, FLIP[k], pl.ds(8, 4, stride=10), :] = g[k][4:8]
-        for i, k in enumerate(OUT):
-            r2e[i, t] = g[k]
+            r2e[k, t] = g[k]
         f = [None] * 19
         for i, k in enumerate(LOCAL):
             f[FLIP[k]] = received(5 + i, t)
@@ -384,35 +399,35 @@
             own = got[IN.index(OPP[k]), t]
             f[k] = stream_rim(lambda s, i=i: edge(i, s), own, k, t, lane, row)
         g = collide(f, force_rim)
-        for i, k in enumerate(IN + FLAT + OUT):
-            r2h[i, t] = g[k]
-            if k in IN:
-                around(r2, t, k, g[k])
+        for k in range(19):
+            r2h[k, t] = g[k]
         for i in range(5):
             got2[i, t] = received(19 + i, t)
 
-    place = {k: i for i, k in enumerate(IN + FLAT + OUT)}
+    def at(ref, index=None):
+        return lambda k, s: ref[k if index is None else index.index(k), s]
 
     for t in range(9):
-        f = [None] * 19
-        for k in range(19):
-            own = r2h[place[OPP[k]], t]
-            if k == 0:
-                f[k] = own
-            elif k in FLAT:
-                f[k] = stream_rim(lambda s, k=k: r2h[place[k], s], own, k, t, lane, row)
-            elif k in IN:
-                f[k] = stream_rim(lambda s, k=k: got2[IN.index(k), s], own, k, t, lane, row)
-            else:
-                f[k] = stream_rim(lambda s, k=k: r2e[OUT.index(k), s], own, k, t, lane, row)
-        g = collide(f, force_rim)
-        for k in IN:
-            around(r3, t, k, g[k])
-        for p in range(4):
-            g = collide(stream_own(load2, p, t, lane), force)
+        for depth, (level, inward, outward) in enumerate(
+            (
+                (at(r2h), at(got2, IN), at(r2e)),
+                (at(r2e), at(r2h), at(second)),
+                (at(second), at(r2e), at(third, OUT)),
+            )
+        ):
+            f = []
             for k in range(19):
-                r3[t, k, pl.ds(10 * p + 1, 8), :] = g[k]
-
+                own = level(OPP[k], t)
+                if k == 0:
+                    f.append(own)
+                    continue
+                src = level if k in FLAT else (inward if k in IN else outward)
+                f.append(stream_rim(lambda s, k=k, src=src: src(k, s), own, k, t, lane, row))
+            g = collide(f, force_rim)
+            for k in IN if depth == 0 else range(19):
+                put(t, k, g[k], depth)
+
+    writes = []
     for t in range(8):
         at = pl.ds(t * 128, 128)
         for p in range(4):
@@ -430,6 +445,16 @@
                 for x, y in zip(plus[1:], minus[1:]):
                     j = j + (x - y)
                 velocity[a, p, :, at] = jnp.where(solid, 0.0, j * inv)
+        if (t + 1) % WRITE == 0:
+            done = pl.ds(128 * (t + 1 - WRITE), 128 * WRITE)
+            writes.append(pltpu.make_async_copy(density.at[:, :, done], density_hbm.at[:, :, done], sem.at[len(writes)]))
+            writes.append(
+                pltpu.make_async_copy(velocity.at[:, :, :, done], velocity_hbm.at[:, :, :, done], sem.at[len(writes)])
+            )
+            for copy in writes[-2:]:
+                copy.start()
+    for copy in writes:
+        copy.wait()
 
 
 VMEM = pl.BlockSpec(memory_space=pltpu.VMEM)
@@ -485,10 +510,11 @@
     got1 = swap(z1, "gz", 1)
     got0 = swap(z0, "gz", 0)
     pop_tiles, mask_tiles = tiles(pop), tiles(mask)
-    e1, e2, e3, inner = call(
+    e1, e2, e3, inner, r1 = call(
         edge_kernel, "edge", 2.0,
-        (sds(19, 64, 128), sds(19, 64, 128), sds(5, 64, 128), sds(6, NMSG, 8, 128)),
-        [VMEM] * 3, (VMEM,) * 4, [],
+        (sds(19, 64, 128), sds(19, 64, 128), sds(5, 64, 128), sds(6, NMSG, 8, 128),
+         sds(OWN, 19, 32, 128)),
+        [VMEM] * 3, (VMEM,) * 5, [],
     )(force, pop_tiles, mask_tiles)
     strip, outer, far, near = call(
         rim_kernel, "rim", 1.0,
@@ -498,17 +524,19 @@
     )(force, e1, e2, e3, inner, got1, got0)
     far = swap(far, "gy", 1)
     near = swap(near, "gy", 0)
-    r2 = call(
+    r3, second, third = call(
         middle_kernel, "middle", 3.0,
-        sds(9, 19, 32, 128), [VMEM] * 4, VMEM, [buf(9, 19, 32, 128)],
-    )(force, pop_tiles, mask_tiles, strip)
+        (sds(9, 19, 32, 128), sds(19, 9, 8, 128), sds(5, 9, 8, 128)), [VMEM] * 5, (VMEM,) * 3,
+        [buf(8 - OWN, 19, 32, 128), buf(19, 32, 128), buf(9, 19, 32, 128)],
+    )(force, pop_tiles, mask_tiles, r1, strip)
     return call(
         last_kernel, "last", 4.0,
         (sds(4, 8, 1024), sds(3, 4, 8, 1024)),
-        [VMEM] * 7, (VMEM, VMEM),
-        [buf(9, 19, 40, 128), buf(9, 19, 40, 128), buf(5, 9, 8, 128), buf(5, 9, 8, 128),
-         buf(19, 9, 8, 128), buf(5, 9, 8, 128)],
-    )(force, r2, inner, outer, far, near, mask)
+        [VMEM] * 9, (HBM, HBM),
+        [buf(9, 19, 40, 128), buf(5, 9, 8, 128), buf(5, 9, 8, 128),
+         buf(19, 9, 8, 128), buf(19, 9, 8, 128), buf(4, 8, 1024), buf(3, 4, 8, 1024),
+         pltpu.SemaphoreType.DMA((16 // WRITE,))],
+    )(force, r3, second, third, inner, outer, far, near, mask)
 
 
 def solution(mesh):

time: 24.5 us -> 24.4 us (level)
  waiting for transfers between devices: 3.78 us -> 2.56 us
  Pallas kernels: 8.72 us -> 9.57 us
  starting transfers between devices: 10.9 us -> 11.3 us
    ppermute x4, waiting for transfers between devices: 3.78 us -> 2.56 us  [swap(): return lax.ppermute(x, axis, pairs)]
    pallas_call x1, Pallas kernels: 2.33 us -> 3.09 us  [local(): call(middle_kernel, 'middle', 3.0, (sds(9, 19, 32, 128), sds(19, 9, 8, 12...]
    ppermute x4, starting transfers between devices: 10.9 us -> 11.3 us  [swap(): return lax.ppermute(x, axis, pairs)]
    pallas_call x1, Pallas kernels: 1.13 us -> 1.58 us  [local(): call(edge_kernel, 'edge', 2.0, (sds(19, 64, 128), sds(19, 64, 128), sds(5...]
    pallas_call x1, Pallas kernels: 3.27 us -> 2.9 us  [local(): call(last_kernel, 'last', 4.0, (sds(4, 8, 1024), sds(3, 4, 8, 1024)), [VM...]
  transfers between devices with their start and end apart: 4 -> 4, of which waited for: 2 -> 2; matrix products, arithmetic and copies ran while one was open for 0% -> 0% of each run, Pallas kernels for 14% -> 19%
where the time goes in v5:
time: 24.4 us; the launch traced here: 24.2 us
  starting transfers between devices  11.3 us (46%)
  Pallas kernels  9.57 us (39%)
  waiting for transfers between devices  2.56 us (10%)
  between operations  0.68 us (3%)
    ppermute x4, starting transfers between devices, swap(): return lax.ppermute(x, axis, pairs)  11.3 us
    pallas_call x1, Pallas kernels, local(): call(middle_kernel, 'middle', 3.0, (sds(9, 19, 32, 128), sds(19, 9, 8, 12...  3.09 us
    pallas_call x1, Pallas kernels, local(): call(last_kernel, 'last', 4.0, (sds(4, 8, 1024), sds(3, 4, 8, 1024)), [VM...  2.9 us
    ppermute x4, waiting for transfers between devices, swap(): return lax.ppermute(x, axis, pairs)  2.56 us
    pallas_call x1, Pallas kernels, local(): call(edge_kernel, 'edge', 2.0, (sds(19, 64, 128), sds(19, 64, 128), sds(5...  1.58 us
    pallas_call x1, Pallas kernels, local(): call(pack_kernel, 'pack', 0.7, (sds(5, 8, 128), sds(5, 8, 128), jax.Shape...  1.55 us
  transfers between devices with their start and end apart: 4, of which 2 were waited for; matrix products, arithmetic and copies ran while one was open for 0% of the time, Pallas kernels for 19%

profile of v5, /device:TPU:8, one launch (start us, length us, event | category | flops | bytes accessed | tf_op | source)
XLA Modules:
  0.0 24.2 jit_solution(12881481961094550221)
XLA Ops:
  0.6 0.0 copy-start
  0.6 1.6 %pack.1 = (f32[5,8,128]{2,1,0:T(8,128)S(1)}, f32[5,8,128]{2,1,0:T(8,128)S(1)}, s32[4,8,1024]{2,1,0:T(8,128)S(1)}, f32[3,8,128]{2,1,0:T(8,128)S(1)}) custom-call(f32[19,4,8,1024]{3,2,1,0:T(8,128)} %pop_hbm.1, s32[4,8,1024]{2,1,0:T(8,128)} %mask_hbm.1, f32[3]{0:T(128)} %force_hbm.1), custom_call_target="tpu_custom_call" | custom-call | flops 700000 | bytes 2100000 | tf_op jit(solution)/shard_map/pack/pallas_call | solution.py:503
  2.2 1.7 %collective-permute-start = (f32[5,8,128]{2,1,0:T(8,128)S(1)}, f32[5,8,128]{2,1,0:T(8,128)S(1)}, u32[]{:S(2)}, u32[]{:S(2)}) collective-permute-start(f32[5,8,128]{2,1,0:T(8,128)S(1)} %get-tuple-element.25), channel_id=1, source_target_pairs={{0,7},{1,2},{2,1},{3,4},{4,3},{5,6},{6,5},{7,0},{8,15},{9,10},{10,... | collective-permute-start | bytes 61448 | tf_op jit(solution)/shard_map/ppermute | solution.py:490
  3.9 2.8 %collective-permute-start.1 = (f32[5,8,128]{2,1,0:T(8,128)S(1)}, f32[5,8,128]{2,1,0:T(8,128)S(1)}, u32[]{:S(2)}, u32[]{:S(2)}) collective-permute-start(f32[5,8,128]{2,1,0:T(8,128)S(1)} %get-tuple-element.26), channel_id=1, source_target_pairs={{0,1},{1,0},{2,3},{3,2},{4,5},{5,4},{6,7},{7,6},{8,9},{9,8},{10,11... | collective-permute-start | bytes 61448 | tf_op jit(solution)/shard_map/ppermute | solution.py:490
  6.7 0.0 copy-done
  6.7 1.6 %edge.1 = (f32[19,64,128]{2,1,0:T(8,128)S(1)}, f32[19,64,128]{2,1,0:T(8,128)S(1)}, f32[5,64,128]{2,1,0:T(8,128)S(1)}, f32[6,24,8,128]{3,2,1,0:T(8,128)S(1)}, f32[4,19,32,128]{3,2,1,0:T(8,128)S(1)}) custom-call(f32[3,8,128]{2,1,0:T(8,128)S(1)} %get-tuple-element.18.force_ref, f32[19,256,128]{2,1,0:T(8,128)S(1)} %bitcast.10, s32[256,128]{1,0:T(8,128)S(1)} %bitcast.12), custom_call_target="tpu_custom_call" | custom-call | flops 2000000 | bytes 6000000 | tf_op jit(solution)/shard_map/edge/pallas_call | solution.py:513
  8.3 0.0 collective-permute-done.got1
  8.3 0.2 collective-permute-done.1.got0
  8.4 0.4 %rim.1 = (f32[19,32,128]{2,1,0:T(8,128)S(1)}, f32[3,19,8,128]{3,2,1,0:T(8,128)S(1)}, f32[194,4,128]{2,1,0:T(4,128)S(1)}, f32[194,4,128]{2,1,0:T(4,128)S(1)}) custom-call(f32[3,8,128]{2,1,0:T(8,128)S(1)} %get-tuple-element.18.force_ref, f32[19,64,128]{2,1,0:T(8,128)S(1)} %get-tuple-element.21.e1, f32[19,64,128]{2,1,0:T(8,128)S(1)} %get-tuple-element.22.e2, ...), custom_call_target="tpu_custom_call" | custom-call | flops 1000000 | bytes 3000000 | tf_op jit(solution)/shard_map/rim/pallas_call | solution.py:519
  8.9 6.9 %collective-permute-start.2 = (f32[194,4,128]{2,1,0:T(4,128)S(1)}, f32[194,4,128]{2,1,0:T(4,128)S(1)}, u32[]{:S(2)}, u32[]{:S(2)}) collective-permute-start(f32[194,4,128]{2,1,0:T(4,128)S(1)} %get-tuple-element.32), channel_id=1, source_target_pairs={{0,248},{8,16},{16,8},{24,32},{32,24},{40,48},{48,40},{56,64},{64,... | collective-permute-start | bytes 1191944 | tf_op jit(solution)/shard_map/ppermute | solution.py:490
  15.7 0.0 collective-permute-start.3
  15.7 3.1 %middle.1 = (f32[9,19,32,128]{3,2,1,0:T(8,128)S(1)}, f32[19,9,8,128]{3,2,1,0:T(8,128)S(1)}, f32[5,9,8,128]{3,2,1,0:T(8,128)S(1)}) custom-call(f32[3,8,128]{2,1,0:T(8,128)S(1)} %get-tuple-element.18.force_ref, f32[19,256,128]{2,1,0:T(8,128)S(1)} %bitcast.11, s32[256,128]{1,0:T(8,128)S(1)} %bitcast.13, f32[4,19,32,128]{3,2,1,0:T(8,128)S(1)} %get-tuple-element.20.r1, ...), custom_call_target="tpu_custom_call" | custom-call | flops 3000000 | bytes 9000000 | tf_op jit(solution)/shard_map/middle/pallas_call | solution.py:527
  18.8 2.4 %collective-permute-done.2.far = f32[194,4,128]{2,1,0:T(4,128)S(1)} collective-permute-done((f32[194,4,128]{2,1,0:T(4,128)S(1)}, f32[194,4,128]{2,1,0:T(4,128)S(1)}, u32[]{:S(2)}, u32[]{:S(2)}) %collective-permute-start.2) | collective-permute-done | bytes 397344 | tf_op jit(solution)/shard_map/ppermute | solution.py:490
  21.2 0.0 collective-permute-done.3.near
  21.3 2.9 %last.1 = (f32[4,8,1024]{2,1,0:T(8,128)}, f32[3,4,8,1024]{3,2,1,0:T(8,128)}) custom-call(f32[3,8,128]{2,1,0:T(8,128)S(1)} %get-tuple-element.18.force_ref, f32[9,19,32,128]{3,2,1,0:T(8,128)S(1)} %get-tuple-element.28.r3_in, f32[19,9,8,128]{3,2,1,0:T(8,128)S(1)} %get-tuple-element.29.second, f32[5,9,8,128]{3,2,1,0:T(8,128)S(1)} %get-tuple-element.30.third, ...), custom_call_target="tpu_custom_call" | custom-call | flops 4000000 | bytes 12000000 | tf_op jit(solution)/shard_map/last/pallas_call | solution.py:532
Async XLA Ops:
  0.6 6.1 %copy-start = (f32[19,4,8,1024]{3,2,1,0:T(8,128)S(1)}, f32[19,4,8,1024]{3,2,1,0:T(8,128)}, u32[]{:S(2)}) copy-start(f32[19,4,8,1024]{3,2,1,0:T(8,128)} %pop_hbm.1) | copy-start | bytes 7471108
  2.2 6.1 %collective-permute-start = (f32[5,8,128]{2,1,0:T(8,128)S(1)}, f32[5,8,128]{2,1,0:T(8,128)S(1)}, u32[]{:S(2)}, u32[]{:S(2)}) collective-permute-start(f32[5,8,128]{2,1,0:T(8,128)S(1)} %get-tuple-element.25), channel_id=1, source_target_pairs={{0,7},{1,2},{2,1},{3,4},{4,3},{5,6},{6,5},{7,0},{8,15},{9,10},{10,... | collective-permute-start | bytes 61448 | tf_op jit(solution)/shard_map/ppermute | solution.py:490
  3.9 4.6 %collective-permute-start.1 = (f32[5,8,128]{2,1,0:T(8,128)S(1)}, f32[5,8,128]{2,1,0:T(8,128)S(1)}, u32[]{:S(2)}, u32[]{:S(2)}) collective-permute-start(f32[5,8,128]{2,1,0:T(8,128)S(1)} %get-tuple-element.26), channel_id=1, source_target_pairs={{0,1},{1,0},{2,3},{3,2},{4,5},{5,4},{6,7},{7,6},{8,9},{9,8},{10,11... | collective-permute-start | bytes 61448 | tf_op jit(solution)/shard_map/ppermute | solution.py:490
  8.9 12.4 %collective-permute-start.2 = (f32[194,4,128]{2,1,0:T(4,128)S(1)}, f32[194,4,128]{2,1,0:T(4,128)S(1)}, u32[]{:S(2)}, u32[]{:S(2)}) collective-permute-start(f32[194,4,128]{2,1,0:T(4,128)S(1)} %get-tuple-element.32), channel_id=1, source_target_pairs={{0,248},{8,16},{16,8},{24,32},{32,24},{40,48},{48,40},{56,64},{64,... | collective-permute-start | bytes 1191944 | tf_op jit(solution)/shard_map/ppermute | solution.py:490
  15.7 5.5 %collective-permute-start.3 = (f32[194,4,128]{2,1,0:T(4,128)S(1)}, f32[194,4,128]{2,1,0:T(4,128)S(1)}, u32[]{:S(2)}, u32[]{:S(2)}) collective-permute-start(f32[194,4,128]{2,1,0:T(4,128)S(1)} %get-tuple-element.33), channel_id=1, source_target_pairs={{0,8},{8,0},{16,24},{24,16},{32,40},{40,32},{48,56},{56,48},{64,72... | collective-permute-start | bytes 1191944 | tf_op jit(solution)/shard_map/ppermute | solution.py:490

commit v6 on v5

--- a/solution.py
+++ b/solution.py
@@ -332,7 +332,8 @@
             for p in range(4):
                 g = collide(stream_own(load, p, t, lane), force)
                 for k in range(19):
-                    after[t, k, 8 * p : 8 * p + 8, :] = g[k]
+                    if t < 8 or after is r2 or VEL[k][2]:
+                        after[t, k, 8 * p : 8 * p + 8, :] = g[k]
 
     for t in range(9):
         for k in range(19):
@@ -382,7 +383,8 @@
     for t in range(9):
         for k in range(19):
             for p in range(4):
-                r3[t, k, pl.ds(10 * p + 1, 8), :] = r3_in[t, k, 8 * p : 8 * p + 8, :]
+                if t < 8 or VEL[k][2]:
+                    r3[t, k, pl.ds(10 * p + 1, 8), :] = r3_in[t, k, 8 * p : 8 * p + 8, :]
         f = [None] * 19
         for i, k in enumerate(LOCAL):
             f[k] = edge(5 + i, t)
@@ -425,7 +427,8 @@
                 f.append(stream_rim(lambda s, k=k, src=src: src(k, s), own, k, t, lane, row))
             g = collide(f, force_rim)
             for k in IN if depth == 0 else range(19):
-                put(t, k, g[k], depth)
+                if t < 8 or VEL[k][2]:
+                    put(t, k, g[k], depth)
 
     writes = []
     for t in range(8):

time: 24.4 us -> 24.3 us (level)
  no operation moved by 1% of the time
where the time goes in v6:
time: 24.3 us; the launch traced here: 24.1 us
  starting transfers between devices  11.3 us (47%)
  Pallas kernels  9.54 us (39%)
  waiting for transfers between devices  2.59 us (11%)
  between operations  0.68 us (3%)
    ppermute x4, starting transfers between devices, swap(): return lax.ppermute(x, axis, pairs)  11.3 us
    pallas_call x1, Pallas kernels, local(): call(middle_kernel, 'middle', 3.0, (sds(9, 19, 32, 128), sds(19, 9, 8, 12...  3.06 us
    pallas_call x1, Pallas kernels, local(): call(last_kernel, 'last', 4.0, (sds(4, 8, 1024), sds(3, 4, 8, 1024)), [VM...  2.9 us
    ppermute x4, waiting for transfers between devices, swap(): return lax.ppermute(x, axis, pairs)  2.59 us
    pallas_call x1, Pallas kernels, local(): call(edge_kernel, 'edge', 2.0, (sds(19, 64, 128), sds(19, 64, 128), sds(5...  1.58 us
    pallas_call x1, Pallas kernels, local(): call(pack_kernel, 'pack', 0.7, (sds(5, 8, 128), sds(5, 8, 128), jax.Shape...  1.55 us
  transfers between devices with their start and end apart: 4, of which 2 were waited for; matrix products, arithmetic and copies ran while one was open for 0% of the time, Pallas kernels for 19%

profile of v6, /device:TPU:8, one launch (start us, length us, event | category | flops | bytes accessed | tf_op | source)
XLA Modules:
  0.0 24.1 jit_solution(3858097695416387018)
XLA Ops:
  0.6 0.0 copy-start
  0.6 1.6 %pack.1 = (f32[5,8,128]{2,1,0:T(8,128)S(1)}, f32[5,8,128]{2,1,0:T(8,128)S(1)}, s32[4,8,1024]{2,1,0:T(8,128)S(1)}, f32[3,8,128]{2,1,0:T(8,128)S(1)}) custom-call(f32[19,4,8,1024]{3,2,1,0:T(8,128)} %pop_hbm.1, s32[4,8,1024]{2,1,0:T(8,128)} %mask_hbm.1, f32[3]{0:T(128)} %force_hbm.1), custom_call_target="tpu_custom_call" | custom-call | flops 700000 | bytes 2100000 | tf_op jit(solution)/shard_map/pack/pallas_call | solution.py:506
  2.2 1.7 %collective-permute-start = (f32[5,8,128]{2,1,0:T(8,128)S(1)}, f32[5,8,128]{2,1,0:T(8,128)S(1)}, u32[]{:S(2)}, u32[]{:S(2)}) collective-permute-start(f32[5,8,128]{2,1,0:T(8,128)S(1)} %get-tuple-element.25), channel_id=1, source_target_pairs={{0,7},{1,2},{2,1},{3,4},{4,3},{5,6},{6,5},{7,0},{8,15},{9,10},{10,... | collective-permute-start | bytes 61448 | tf_op jit(solution)/shard_map/ppermute | solution.py:493
  3.9 2.8 %collective-permute-start.1 = (f32[5,8,128]{2,1,0:T(8,128)S(1)}, f32[5,8,128]{2,1,0:T(8,128)S(1)}, u32[]{:S(2)}, u32[]{:S(2)}) collective-permute-start(f32[5,8,128]{2,1,0:T(8,128)S(1)} %get-tuple-element.26), channel_id=1, source_target_pairs={{0,1},{1,0},{2,3},{3,2},{4,5},{5,4},{6,7},{7,6},{8,9},{9,8},{10,11... | collective-permute-start | bytes 61448 | tf_op jit(solution)/shard_map/ppermute | solution.py:493
  6.7 0.0 copy-done
  6.7 1.6 %edge.1 = (f32[19,64,128]{2,1,0:T(8,128)S(1)}, f32[19,64,128]{2,1,0:T(8,128)S(1)}, f32[5,64,128]{2,1,0:T(8,128)S(1)}, f32[6,24,8,128]{3,2,1,0:T(8,128)S(1)}, f32[4,19,32,128]{3,2,1,0:T(8,128)S(1)}) custom-call(f32[3,8,128]{2,1,0:T(8,128)S(1)} %get-tuple-element.18.force_ref, f32[19,256,128]{2,1,0:T(8,128)S(1)} %bitcast.10, s32[256,128]{1,0:T(8,128)S(1)} %bitcast.12), custom_call_target="tpu_custom_call" | custom-call | flops 2000000 | bytes 6000000 | tf_op jit(solution)/shard_map/edge/pallas_call | solution.py:516
  8.3 0.0 collective-permute-done.got1
  8.3 0.2 collective-permute-done.1.got0
  8.4 0.4 %rim.1 = (f32[19,32,128]{2,1,0:T(8,128)S(1)}, f32[3,19,8,128]{3,2,1,0:T(8,128)S(1)}, f32[194,4,128]{2,1,0:T(4,128)S(1)}, f32[194,4,128]{2,1,0:T(4,128)S(1)}) custom-call(f32[3,8,128]{2,1,0:T(8,128)S(1)} %get-tuple-element.18.force_ref, f32[19,64,128]{2,1,0:T(8,128)S(1)} %get-tuple-element.21.e1, f32[19,64,128]{2,1,0:T(8,128)S(1)} %get-tuple-element.22.e2, ...), custom_call_target="tpu_custom_call" | custom-call | flops 1000000 | bytes 3000000 | tf_op jit(solution)/shard_map/rim/pallas_call | solution.py:522
  8.9 6.9 %collective-permute-start.2 = (f32[194,4,128]{2,1,0:T(4,128)S(1)}, f32[194,4,128]{2,1,0:T(4,128)S(1)}, u32[]{:S(2)}, u32[]{:S(2)}) collective-permute-start(f32[194,4,128]{2,1,0:T(4,128)S(1)} %get-tuple-element.32), channel_id=1, source_target_pairs={{0,248},{8,16},{16,8},{24,32},{32,24},{40,48},{48,40},{56,64},{64,... | collective-permute-start | bytes 1191944 | tf_op jit(solution)/shard_map/ppermute | solution.py:493
  15.7 0.0 collective-permute-start.3
  15.7 3.1 %middle.1 = (f32[9,19,32,128]{3,2,1,0:T(8,128)S(1)}, f32[19,9,8,128]{3,2,1,0:T(8,128)S(1)}, f32[5,9,8,128]{3,2,1,0:T(8,128)S(1)}) custom-call(f32[3,8,128]{2,1,0:T(8,128)S(1)} %get-tuple-element.18.force_ref, f32[19,256,128]{2,1,0:T(8,128)S(1)} %bitcast.11, s32[256,128]{1,0:T(8,128)S(1)} %bitcast.13, f32[4,19,32,128]{3,2,1,0:T(8,128)S(1)} %get-tuple-element.20.r1, ...), custom_call_target="tpu_custom_call" | custom-call | flops 3000000 | bytes 9000000 | tf_op jit(solution)/shard_map/middle/pallas_call | solution.py:530
  18.8 2.4 %collective-permute-done.2.far = f32[194,4,128]{2,1,0:T(4,128)S(1)} collective-permute-done((f32[194,4,128]{2,1,0:T(4,128)S(1)}, f32[194,4,128]{2,1,0:T(4,128)S(1)}, u32[]{:S(2)}, u32[]{:S(2)}) %collective-permute-start.2) | collective-permute-done | bytes 397344 | tf_op jit(solution)/shard_map/ppermute | solution.py:493
  21.2 0.0 collective-permute-done.3.near
  21.3 2.9 %last.1 = (f32[4,8,1024]{2,1,0:T(8,128)}, f32[3,4,8,1024]{3,2,1,0:T(8,128)}) custom-call(f32[3,8,128]{2,1,0:T(8,128)S(1)} %get-tuple-element.18.force_ref, f32[9,19,32,128]{3,2,1,0:T(8,128)S(1)} %get-tuple-element.28.r3_in, f32[19,9,8,128]{3,2,1,0:T(8,128)S(1)} %get-tuple-element.29.second, f32[5,9,8,128]{3,2,1,0:T(8,128)S(1)} %get-tuple-element.30.third, ...), custom_call_target="tpu_custom_call" | custom-call | flops 4000000 | bytes 12000000 | tf_op jit(solution)/shard_map/last/pallas_call | solution.py:535
Async XLA Ops:
  0.6 6.1 %copy-start = (f32[19,4,8,1024]{3,2,1,0:T(8,128)S(1)}, f32[19,4,8,1024]{3,2,1,0:T(8,128)}, u32[]{:S(2)}) copy-start(f32[19,4,8,1024]{3,2,1,0:T(8,128)} %pop_hbm.1) | copy-start | bytes 7471108
  2.2 6.1 %collective-permute-start = (f32[5,8,128]{2,1,0:T(8,128)S(1)}, f32[5,8,128]{2,1,0:T(8,128)S(1)}, u32[]{:S(2)}, u32[]{:S(2)}) collective-permute-start(f32[5,8,128]{2,1,0:T(8,128)S(1)} %get-tuple-element.25), channel_id=1, source_target_pairs={{0,7},{1,2},{2,1},{3,4},{4,3},{5,6},{6,5},{7,0},{8,15},{9,10},{10,... | collective-permute-start | bytes 61448 | tf_op jit(solution)/shard_map/ppermute | solution.py:493
  3.9 4.6 %collective-permute-start.1 = (f32[5,8,128]{2,1,0:T(8,128)S(1)}, f32[5,8,128]{2,1,0:T(8,128)S(1)}, u32[]{:S(2)}, u32[]{:S(2)}) collective-permute-start(f32[5,8,128]{2,1,0:T(8,128)S(1)} %get-tuple-element.26), channel_id=1, source_target_pairs={{0,1},{1,0},{2,3},{3,2},{4,5},{5,4},{6,7},{7,6},{8,9},{9,8},{10,11... | collective-permute-start | bytes 61448 | tf_op jit(solution)/shard_map/ppermute | solution.py:493
  8.9 12.4 %collective-permute-start.2 = (f32[194,4,128]{2,1,0:T(4,128)S(1)}, f32[194,4,128]{2,1,0:T(4,128)S(1)}, u32[]{:S(2)}, u32[]{:S(2)}) collective-permute-start(f32[194,4,128]{2,1,0:T(4,128)S(1)} %get-tuple-element.32), channel_id=1, source_target_pairs={{0,248},{8,16},{16,8},{24,32},{32,24},{40,48},{48,40},{56,64},{64,... | collective-permute-start | bytes 1191944 | tf_op jit(solution)/shard_map/ppermute | solution.py:493
  15.7 5.5 %collective-permute-start.3 = (f32[194,4,128]{2,1,0:T(4,128)S(1)}, f32[194,4,128]{2,1,0:T(4,128)S(1)}, u32[]{:S(2)}, u32[]{:S(2)}) collective-permute-start(f32[194,4,128]{2,1,0:T(4,128)S(1)} %get-tuple-element.33), channel_id=1, source_target_pairs={{0,8},{8,0},{16,24},{24,16},{32,40},{40,32},{48,56},{56,48},{64,72... | collective-permute-start | bytes 1191944 | tf_op jit(solution)/shard_map/ppermute | solution.py:493
